TPU v7x, 512 devices: a whole 4x8x8 slice. The times are simulated.
512 devices in a mesh: sky: 64 (over z, y_hi, core), epoch: 8 (over y_lo, x).
Axes of the slice: x: 4, y: 8 (y_hi: 4, y_lo: 2; y = y_hi * 2 + y_lo), z: 8, core: 2. Of those that a mesh axis runs over, the one named last changes fastest.
Arguments:
- visits: float32 [8, 8192, 1024], P('epoch', 'sky'), may hold values from -6 to 6
- template: float32 [8192, 1024], P(('sky', 'epoch')), may hold values from -6 to 6
- basis_taps: float32 [2, 27, 17], replicated, may hold values from -1.5 to 1.5
- coeffs: float32 [8, 64, 27, 3], P('epoch', 'sky'), may hold values from -1.2 to 1.2
- psf_taps: float32 [8, 9], P('epoch'), may hold values from -2 to 2
- inv_var: float32 [8, 8192, 1024], P('epoch', 'sky'), may hold values from 0.3 to 3
- shifts: int32 [64, 24, 8, 2], P('sky'), may hold values from -16 to 16
- vel_count: int32 [64], P('sky'), may hold values from 1 to 24, 768 in all
Outputs:
- best_map: float32 [8192, 1024], P(('sky', 'epoch'))
Inputs may be any that keep to these rules, and one draw needn't show every extreme that they name: `shifts`: a velocity's shift of one epoch, row first, in whole pixels. Velocities 0 to vel_count - 1 of a tile are searched; some tile searches all 24.
All inputs are finite; a program needn't handle non-finite values. No bound on the sum of `vel_count` on one device may be relied on, other than what follows from the above.
Results may differ from a plain program's by a relative error of at most 0.0026.
Values may be sent and summed in bfloat16 or wider, within the bound.
No kernel may reach another device: no remote copies, remote signals or barrier semaphores. Data moves between devices by JAX's collectives and lax.ppermute only.
A program may use at most 64 MiB of HBM per device.

v0:
```python
import jax
import jax.numpy as jnp
from jax import lax
from jax.sharding import PartitionSpec as P

NB = 27
R = 8
F = 4
SMAX = 16


def padded_2(cells, sides, width):
    for axis, dim in sides:
        count = lax.axis_size(axis)
        ends = count - 1
        head = lax.slice_in_dim(cells, 0, width, axis=dim)
        tail = lax.slice_in_dim(cells, cells.shape[dim] - width, cells.shape[dim], axis=dim)
        cells = jnp.concatenate(
            [
                lax.ppermute(tail, axis, [(i, (i + 1) % count) for i in range(ends)]),
                cells,
                lax.ppermute(head, axis, [((i + 1) % count, i) for i in range(ends)]),
            ],
            axis=dim,
        )
    return cells


def conv_rows(extended, kernel, half_width):
    height = extended.shape[0] - 2 * half_width
    result = kernel[0] * extended[0:height]
    for offset in range(1, 2 * half_width + 1):
        result = result + kernel[offset] * extended[offset : offset + height]
    return result


def conv_cols(image, kernel, half_width):
    columns = image.shape[1]
    padded = jnp.pad(image, ((0, 0), (half_width, half_width)))
    result = kernel[0] * padded[:, 0:columns]
    for offset in range(1, 2 * half_width + 1):
        result = result + kernel[offset] * padded[:, offset : offset + columns]
    return result


def normalized(position, length):
    return (position - (length - 1) / 2.0) / ((length - 1) / 2.0)


def stack_window(padded, shift_table, height, columns, epochs):
    total = jnp.zeros((height, columns), jnp.float32)
    for epoch_index in range(epochs):
        window = lax.dynamic_slice(
            padded[epoch_index],
            (SMAX + shift_table[epoch_index, 0], SMAX + shift_table[epoch_index, 1]),
            (height, columns),
        )
        total = total + window.astype(jnp.float32)
    return total


def on_device(visits, template, basis_taps, coeffs, psf_taps, inv_var, shifts, vel_count):
    epochs = lax.axis_size("epoch")
    height = visits.shape[1]
    columns = visits.shape[2]
    extended = padded_2(template, ((("sky", "epoch"), 0),), R)
    band_maps = jnp.stack(
        [
            conv_cols(
                conv_rows(extended, basis_taps[0, basis_index], R), basis_taps[1, basis_index], R
            )
            for basis_index in range(NB)
        ]
    )
    gathered_maps = lax.all_gather(band_maps, "epoch", axis=1, tiled=True)
    basis_maps = [gathered_maps[basis_index] for basis_index in range(NB)]
    row_pos = normalized(jnp.arange(height, dtype=jnp.int32).astype(jnp.float32), height)[:, None]
    col_pos = normalized(jnp.arange(columns, dtype=jnp.int32).astype(jnp.float32), columns)[None, :]
    model = jnp.zeros((height, columns), jnp.float32)
    for basis_index in range(NB):
        spatial = (
            coeffs[0, 0, basis_index, 0]
            + coeffs[0, 0, basis_index, 1] * col_pos
            + coeffs[0, 0, basis_index, 2] * row_pos
        )
        model = model + spatial * basis_maps[basis_index]
    difference = visits[0] - model
    diff_ext = padded_2(difference, (("sky", 0),), F)
    smoothed = conv_cols(conv_rows(diff_ext, psf_taps[0], F), psf_taps[0], F)
    filtered = (smoothed * inv_var[0]).astype(jnp.bfloat16)
    psf_power = jnp.sum(psf_taps[0] * psf_taps[0])
    weight_local = psf_power * psf_power * jnp.mean(inv_var[0])
    scale_norm = jnp.sqrt(lax.psum(weight_local, "epoch"))
    vel_total = vel_count[0]
    shift_list = shifts[0]
    margins = ((0, 0), (0, 0), (SMAX, SMAX))
    every_epoch = lax.all_gather(filtered[None], "epoch", axis=0, tiled=True)
    padded = jnp.pad(padded_2(every_epoch, (("sky", 1),), SMAX), margins)
    epoch_index = lax.axis_index("epoch")
    own_turns = (vel_total - epoch_index + epochs - 1) // epochs

    def visit_own(turn, best_map):
        vel_index = epoch_index + epochs * turn
        candidate = (
            stack_window(padded, shift_list[vel_index], height, columns, epochs) / scale_norm
        )
        return jnp.maximum(best_map, candidate)

    local_best = lax.fori_loop(
        0, own_turns, visit_own, jnp.full((height, columns), -1e30, jnp.float32)
    )
    pieces = lax.all_to_all(local_best[None], "epoch", split_axis=1, concat_axis=0, tiled=True)
    return jnp.max(pieces, axis=0)


def solution(mesh):
    in_specs = (
        P("epoch", "sky", None),
        P(("sky", "epoch"), None),
        P(),
        P("epoch", "sky", None, None),
        P("epoch", None),
        P("epoch", "sky", None),
        P("sky", None, None, None),
        P("sky"),
    )
    out_specs = P(("sky", "epoch"), None)
    return jax.shard_map(
        on_device, mesh=mesh, in_specs=in_specs, out_specs=out_specs, check_vma=False
    )
```

profile of v0, /device:TPU:256, one launch (start us, length us, event | category | flops | bytes accessed | tf_op | source)
XLA Modules:
  0.0 1031.4 jit_solution(1505463107460871998)
XLA Ops:
  10.8 7.6 collective-permute-start.1
  98.3 11.3 %multiply_add_fusion.26 = f32[16,1024]{1,0:T(8,128)S(1)} fusion(f32[16,1024]{1,0:T(8,128)} %param.11, f32[]{:T(128)} %bitcast.57, f32[]{:T(128)} %bitcast.56, f32[]{:T(128)} %bitcast.55, f32[]{:T(128)} %bitcast.54, f32[]{:T(128)} %bitcast.53, f32[]{:T(128)} %bitcast.52, f32[]{:T(128)} %bitcast.51, f32[]{:T(128)} %bitcast.50, f32[]{:T(128)} %bitcast.49, ...), kind=kLoop, calls=%fused_computation.1503 | loop fusion | flops 540672 | bytes 1179716 | tf_op jit(solution)/shard_map/add | solution.py:33
  109.6 11.0 %multiply_add_fusion.25 = f32[16,1024]{1,0:T(8,128)S(1)} fusion(f32[16,1024]{1,0:T(8,128)S(1)} %copy-done, f32[]{:T(128)} %bitcast.92, f32[]{:T(128)} %bitcast.91, f32[]{:T(128)} %bitcast.90, f32[]{:T(128)} %bitcast.89, f32[]{:T(128)} %bitcast.88, f32[]{:T(128)} %bitcast.87, f32[]{:T(128)} %bitcast.86, f32[]{:T(128)} %bitcast.85, f32[]{:T(128)} %bitcast.84, ...), kind=kLoop, calls=%fused_computation.1502 | loop fusion | flops 540672 | bytes 1179716 | tf_op jit(solution)/shard_map/add | solution.py:33
  120.6 10.8 %multiply_add_fusion.24 = f32[16,1024]{1,0:T(8,128)S(1)} fusion(f32[16,1024]{1,0:T(8,128)S(1)} %copy-done, f32[]{:T(128)} %bitcast.127, f32[]{:T(128)} %bitcast.126, f32[]{:T(128)} %bitcast.125, f32[]{:T(128)} %bitcast.124, f32[]{:T(128)} %bitcast.123, f32[]{:T(128)} %bitcast.122, f32[]{:T(128)} %bitcast.121, f32[]{:T(128)} %bitcast.120, f32[]{:T(128)} %bitcast.119, ...), kind=kLoop, calls=%fused_computation.1501 | loop fusion | flops 540672 | bytes 1179716 | tf_op jit(solution)/shard_map/add | solution.py:33
  131.4 10.6 %multiply_add_fusion.23 = f32[16,1024]{1,0:T(8,128)S(1)} fusion(f32[16,1024]{1,0:T(8,128)S(1)} %copy-done, f32[]{:T(128)} %bitcast.162, f32[]{:T(128)} %bitcast.161, f32[]{:T(128)} %bitcast.160, f32[]{:T(128)} %bitcast.159, f32[]{:T(128)} %bitcast.158, f32[]{:T(128)} %bitcast.157, f32[]{:T(128)} %bitcast.156, f32[]{:T(128)} %bitcast.155, f32[]{:T(128)} %bitcast.154, ...), kind=kLoop, calls=%fused_computation.1500 | loop fusion | flops 540672 | bytes 1179716 | tf_op jit(solution)/shard_map/add | solution.py:33
  142.0 10.7 %multiply_add_fusion.22 = f32[16,1024]{1,0:T(8,128)S(1)} fusion(f32[16,1024]{1,0:T(8,128)S(1)} %copy-done, f32[]{:T(128)} %bitcast.197, f32[]{:T(128)} %bitcast.196, f32[]{:T(128)} %bitcast.195, f32[]{:T(128)} %bitcast.194, f32[]{:T(128)} %bitcast.193, f32[]{:T(128)} %bitcast.192, f32[]{:T(128)} %bitcast.191, f32[]{:T(128)} %bitcast.190, f32[]{:T(128)} %bitcast.189, ...), kind=kLoop, calls=%fused_computation.1499 | loop fusion | flops 540672 | bytes 1179716 | tf_op jit(solution)/shard_map/add | solution.py:33
  152.7 10.6 %multiply_add_fusion.21 = f32[16,1024]{1,0:T(8,128)S(1)} fusion(f32[16,1024]{1,0:T(8,128)S(1)} %copy-done, f32[]{:T(128)} %bitcast.232, f32[]{:T(128)} %bitcast.231, f32[]{:T(128)} %bitcast.230, f32[]{:T(128)} %bitcast.229, f32[]{:T(128)} %bitcast.228, f32[]{:T(128)} %bitcast.227, f32[]{:T(128)} %bitcast.226, f32[]{:T(128)} %bitcast.225, f32[]{:T(128)} %bitcast.224, ...), kind=kLoop, calls=%fused_computation.1498 | loop fusion | flops 540672 | bytes 1179716 | tf_op jit(solution)/shard_map/add | solution.py:33
  163.3 10.5 %multiply_add_fusion.20 = f32[16,1024]{1,0:T(8,128)S(1)} fusion(f32[16,1024]{1,0:T(8,128)S(1)} %copy-done, f32[]{:T(128)} %bitcast.267, f32[]{:T(128)} %bitcast.266, f32[]{:T(128)} %bitcast.265, f32[]{:T(128)} %bitcast.264, f32[]{:T(128)} %bitcast.263, f32[]{:T(128)} %bitcast.262, f32[]{:T(128)} %bitcast.261, f32[]{:T(128)} %bitcast.260, f32[]{:T(128)} %bitcast.259, ...), kind=kLoop, calls=%fused_computation.1497 | loop fusion | flops 540672 | bytes 1179716 | tf_op jit(solution)/shard_map/add | solution.py:33
  173.8 10.6 %multiply_add_fusion.19 = f32[16,1024]{1,0:T(8,128)S(1)} fusion(f32[16,1024]{1,0:T(8,128)S(1)} %copy-done, f32[]{:T(128)} %bitcast.302, f32[]{:T(128)} %bitcast.301, f32[]{:T(128)} %bitcast.300, f32[]{:T(128)} %bitcast.299, f32[]{:T(128)} %bitcast.298, f32[]{:T(128)} %bitcast.297, f32[]{:T(128)} %bitcast.296, f32[]{:T(128)} %bitcast.295, f32[]{:T(128)} %bitcast.294, ...), kind=kLoop, calls=%fused_computation.1496 | loop fusion | flops 540672 | bytes 1179716 | tf_op jit(solution)/shard_map/add | solution.py:33
  184.4 10.9 %multiply_add_fusion.18 = f32[16,1024]{1,0:T(8,128)S(1)} fusion(f32[16,1024]{1,0:T(8,128)S(1)} %copy-done, f32[]{:T(128)} %bitcast.337, f32[]{:T(128)} %bitcast.336, f32[]{:T(128)} %bitcast.335, f32[]{:T(128)} %bitcast.334, f32[]{:T(128)} %bitcast.333, f32[]{:T(128)} %bitcast.332, f32[]{:T(128)} %bitcast.331, f32[]{:T(128)} %bitcast.330, f32[]{:T(128)} %bitcast.329, ...), kind=kLoop, calls=%fused_computation.1495 | loop fusion | flops 540672 | bytes 1179716 | tf_op jit(solution)/shard_map/add | solution.py:33
  195.3 10.7 %multiply_add_fusion.17 = f32[16,1024]{1,0:T(8,128)S(1)} fusion(f32[16,1024]{1,0:T(8,128)S(1)} %copy-done, f32[]{:T(128)} %bitcast.372, f32[]{:T(128)} %bitcast.371, f32[]{:T(128)} %bitcast.370, f32[]{:T(128)} %bitcast.369, f32[]{:T(128)} %bitcast.368, f32[]{:T(128)} %bitcast.367, f32[]{:T(128)} %bitcast.366, f32[]{:T(128)} %bitcast.365, f32[]{:T(128)} %bitcast.364, ...), kind=kLoop, calls=%fused_computation.1494 | loop fusion | flops 540672 | bytes 1179716 | tf_op jit(solution)/shard_map/add | solution.py:33
  206.0 10.7 %multiply_add_fusion.16 = f32[16,1024]{1,0:T(8,128)S(1)} fusion(f32[16,1024]{1,0:T(8,128)S(1)} %copy-done, f32[]{:T(128)} %bitcast.407, f32[]{:T(128)} %bitcast.406, f32[]{:T(128)} %bitcast.405, f32[]{:T(128)} %bitcast.404, f32[]{:T(128)} %bitcast.403, f32[]{:T(128)} %bitcast.402, f32[]{:T(128)} %bitcast.401, f32[]{:T(128)} %bitcast.400, f32[]{:T(128)} %bitcast.399, ...), kind=kLoop, calls=%fused_computation.1493 | loop fusion | flops 540672 | bytes 1179716 | tf_op jit(solution)/shard_map/add | solution.py:33
  216.7 10.7 %multiply_add_fusion.15 = f32[16,1024]{1,0:T(8,128)S(1)} fusion(f32[16,1024]{1,0:T(8,128)S(1)} %copy-done, f32[]{:T(128)} %bitcast.442, f32[]{:T(128)} %bitcast.441, f32[]{:T(128)} %bitcast.440, f32[]{:T(128)} %bitcast.439, f32[]{:T(128)} %bitcast.438, f32[]{:T(128)} %bitcast.437, f32[]{:T(128)} %bitcast.436, f32[]{:T(128)} %bitcast.435, f32[]{:T(128)} %bitcast.434, ...), kind=kLoop, calls=%fused_computation.1492 | loop fusion | flops 540672 | bytes 1179716 | tf_op jit(solution)/shard_map/add | solution.py:33
  227.5 10.5 %multiply_add_fusion.14 = f32[16,1024]{1,0:T(8,128)S(1)} fusion(f32[16,1024]{1,0:T(8,128)S(1)} %copy-done, f32[]{:T(128)} %bitcast.477, f32[]{:T(128)} %bitcast.476, f32[]{:T(128)} %bitcast.475, f32[]{:T(128)} %bitcast.474, f32[]{:T(128)} %bitcast.473, f32[]{:T(128)} %bitcast.472, f32[]{:T(128)} %bitcast.471, f32[]{:T(128)} %bitcast.470, f32[]{:T(128)} %bitcast.469, ...), kind=kLoop, calls=%fused_computation.1491 | loop fusion | flops 540672 | bytes 1179716 | tf_op jit(solution)/shard_map/add | solution.py:33
  238.0 10.7 %multiply_add_fusion.13 = f32[16,1024]{1,0:T(8,128)S(1)} fusion(f32[16,1024]{1,0:T(8,128)S(1)} %copy-done, f32[]{:T(128)} %bitcast.512, f32[]{:T(128)} %bitcast.511, f32[]{:T(128)} %bitcast.510, f32[]{:T(128)} %bitcast.509, f32[]{:T(128)} %bitcast.508, f32[]{:T(128)} %bitcast.507, f32[]{:T(128)} %bitcast.506, f32[]{:T(128)} %bitcast.505, f32[]{:T(128)} %bitcast.504, ...), kind=kLoop, calls=%fused_computation.1490 | loop fusion | flops 540672 | bytes 1179716 | tf_op jit(solution)/shard_map/add | solution.py:33
  248.7 10.6 %multiply_add_fusion.12 = f32[16,1024]{1,0:T(8,128)S(1)} fusion(f32[16,1024]{1,0:T(8,128)S(1)} %copy-done, f32[]{:T(128)} %bitcast.547, f32[]{:T(128)} %bitcast.546, f32[]{:T(128)} %bitcast.545, f32[]{:T(128)} %bitcast.544, f32[]{:T(128)} %bitcast.543, f32[]{:T(128)} %bitcast.542, f32[]{:T(128)} %bitcast.541, f32[]{:T(128)} %bitcast.540, f32[]{:T(128)} %bitcast.539, ...), kind=kLoop, calls=%fused_computation.1489 | loop fusion | flops 540672 | bytes 1179716 | tf_op jit(solution)/shard_map/add | solution.py:33
  259.3 10.7 %multiply_add_fusion.11 = f32[16,1024]{1,0:T(8,128)S(1)} fusion(f32[16,1024]{1,0:T(8,128)S(1)} %copy-done, f32[]{:T(128)} %bitcast.582, f32[]{:T(128)} %bitcast.581, f32[]{:T(128)} %bitcast.580, f32[]{:T(128)} %bitcast.579, f32[]{:T(128)} %bitcast.578, f32[]{:T(128)} %bitcast.577, f32[]{:T(128)} %bitcast.576, f32[]{:T(128)} %bitcast.575, f32[]{:T(128)} %bitcast.574, ...), kind=kLoop, calls=%fused_computation.1488 | loop fusion | flops 540672 | bytes 1179716 | tf_op jit(solution)/shard_map/add | solution.py:33
  270.0 10.3 multiply_add_fusion.10
  280.3 10.7 %multiply_add_fusion.9 = f32[16,1024]{1,0:T(8,128)S(1)} fusion(f32[16,1024]{1,0:T(8,128)S(1)} %copy-done, f32[]{:T(128)} %bitcast.652, f32[]{:T(128)} %bitcast.651, f32[]{:T(128)} %bitcast.650, f32[]{:T(128)} %bitcast.649, f32[]{:T(128)} %bitcast.648, f32[]{:T(128)} %bitcast.647, f32[]{:T(128)} %bitcast.646, f32[]{:T(128)} %bitcast.645, f32[]{:T(128)} %bitcast.644, ...), kind=kLoop, calls=%fused_computation.1486 | loop fusion | flops 540672 | bytes 1179716 | tf_op jit(solution)/shard_map/add | solution.py:33
  291.0 10.7 %multiply_add_fusion.8 = f32[16,1024]{1,0:T(8,128)S(1)} fusion(f32[16,1024]{1,0:T(8,128)S(1)} %copy-done, f32[]{:T(128)} %bitcast.687, f32[]{:T(128)} %bitcast.686, f32[]{:T(128)} %bitcast.685, f32[]{:T(128)} %bitcast.684, f32[]{:T(128)} %bitcast.683, f32[]{:T(128)} %bitcast.682, f32[]{:T(128)} %bitcast.681, f32[]{:T(128)} %bitcast.680, f32[]{:T(128)} %bitcast.679, ...), kind=kLoop, calls=%fused_computation.1485 | loop fusion | flops 540672 | bytes 1179716 | tf_op jit(solution)/shard_map/add | solution.py:33
  301.7 11.0 %multiply_add_fusion.7 = f32[16,1024]{1,0:T(8,128)S(1)} fusion(f32[16,1024]{1,0:T(8,128)S(1)} %copy-done, f32[]{:T(128)} %bitcast.722, f32[]{:T(128)} %bitcast.721, f32[]{:T(128)} %bitcast.720, f32[]{:T(128)} %bitcast.719, f32[]{:T(128)} %bitcast.718, f32[]{:T(128)} %bitcast.717, f32[]{:T(128)} %bitcast.716, f32[]{:T(128)} %bitcast.715, f32[]{:T(128)} %bitcast.714, ...), kind=kLoop, calls=%fused_computation.1484 | loop fusion | flops 540672 | bytes 1179716 | tf_op jit(solution)/shard_map/add | solution.py:33
  312.7 11.1 %multiply_add_fusion.6 = f32[16,1024]{1,0:T(8,128)S(1)} fusion(f32[16,1024]{1,0:T(8,128)S(1)} %copy-done, f32[]{:T(128)} %bitcast.757, f32[]{:T(128)} %bitcast.756, f32[]{:T(128)} %bitcast.755, f32[]{:T(128)} %bitcast.754, f32[]{:T(128)} %bitcast.753, f32[]{:T(128)} %bitcast.752, f32[]{:T(128)} %bitcast.751, f32[]{:T(128)} %bitcast.750, f32[]{:T(128)} %bitcast.749, ...), kind=kLoop, calls=%fused_computation.1483 | loop fusion | flops 540672 | bytes 1179716 | tf_op jit(solution)/shard_map/add | solution.py:33
  323.8 11.0 %multiply_add_fusion.5 = f32[16,1024]{1,0:T(8,128)S(1)} fusion(f32[16,1024]{1,0:T(8,128)S(1)} %copy-done, f32[]{:T(128)} %bitcast.792, f32[]{:T(128)} %bitcast.791, f32[]{:T(128)} %bitcast.790, f32[]{:T(128)} %bitcast.789, f32[]{:T(128)} %bitcast.788, f32[]{:T(128)} %bitcast.787, f32[]{:T(128)} %bitcast.786, f32[]{:T(128)} %bitcast.785, f32[]{:T(128)} %bitcast.784, ...), kind=kLoop, calls=%fused_computation.1482 | loop fusion | flops 540672 | bytes 1179716 | tf_op jit(solution)/shard_map/add | solution.py:33
  334.7 10.9 %multiply_add_fusion.4 = f32[16,1024]{1,0:T(8,128)S(1)} fusion(f32[16,1024]{1,0:T(8,128)S(1)} %copy-done, f32[]{:T(128)} %bitcast.827, f32[]{:T(128)} %bitcast.826, f32[]{:T(128)} %bitcast.825, f32[]{:T(128)} %bitcast.824, f32[]{:T(128)} %bitcast.823, f32[]{:T(128)} %bitcast.822, f32[]{:T(128)} %bitcast.821, f32[]{:T(128)} %bitcast.820, f32[]{:T(128)} %bitcast.819, ...), kind=kLoop, calls=%fused_computation.1481 | loop fusion | flops 540672 | bytes 1179716 | tf_op jit(solution)/shard_map/add | solution.py:33
  345.6 10.5 %multiply_add_fusion.3 = f32[16,1024]{1,0:T(8,128)S(1)} fusion(f32[16,1024]{1,0:T(8,128)S(1)} %copy-done, f32[]{:T(128)} %bitcast.862, f32[]{:T(128)} %bitcast.861, f32[]{:T(128)} %bitcast.860, f32[]{:T(128)} %bitcast.859, f32[]{:T(128)} %bitcast.858, f32[]{:T(128)} %bitcast.857, f32[]{:T(128)} %bitcast.856, f32[]{:T(128)} %bitcast.855, f32[]{:T(128)} %bitcast.854, ...), kind=kLoop, calls=%fused_computation.1480 | loop fusion | flops 540672 | bytes 1179716 | tf_op jit(solution)/shard_map/add | solution.py:33
  356.1 10.6 %multiply_add_fusion.2 = f32[16,1024]{1,0:T(8,128)S(1)} fusion(f32[16,1024]{1,0:T(8,128)S(1)} %copy-done, f32[]{:T(128)} %bitcast.897, f32[]{:T(128)} %bitcast.896, f32[]{:T(128)} %bitcast.895, f32[]{:T(128)} %bitcast.894, f32[]{:T(128)} %bitcast.893, f32[]{:T(128)} %bitcast.892, f32[]{:T(128)} %bitcast.891, f32[]{:T(128)} %bitcast.890, f32[]{:T(128)} %bitcast.889, ...), kind=kLoop, calls=%fused_computation.1479 | loop fusion | flops 540672 | bytes 1179716 | tf_op jit(solution)/shard_map/add | solution.py:33
  366.8 10.7 %multiply_add_fusion.1 = f32[16,1024]{1,0:T(8,128)S(1)} fusion(f32[16,1024]{1,0:T(8,128)S(1)} %copy-done, f32[]{:T(128)} %bitcast.932, f32[]{:T(128)} %bitcast.931, f32[]{:T(128)} %bitcast.930, f32[]{:T(128)} %bitcast.929, f32[]{:T(128)} %bitcast.928, f32[]{:T(128)} %bitcast.927, f32[]{:T(128)} %bitcast.926, f32[]{:T(128)} %bitcast.925, f32[]{:T(128)} %bitcast.924, ...), kind=kLoop, calls=%fused_computation.1478 | loop fusion | flops 540672 | bytes 1179716 | tf_op jit(solution)/shard_map/add | solution.py:33
  377.5 10.7 %multiply_add_fusion = f32[16,1024]{1,0:T(8,128)S(1)} fusion(f32[16,1024]{1,0:T(8,128)S(1)} %copy-done, f32[]{:T(128)} %bitcast.967, f32[]{:T(128)} %bitcast.966, f32[]{:T(128)} %bitcast.965, f32[]{:T(128)} %bitcast.964, f32[]{:T(128)} %bitcast.963, f32[]{:T(128)} %bitcast.962, f32[]{:T(128)} %bitcast.961, f32[]{:T(128)} %bitcast.960, f32[]{:T(128)} %bitcast.959, ...), kind=kLoop, calls=%fused_computation.1477 | loop fusion | flops 540672 | bytes 1179716 | tf_op jit(solution)/shard_map/add | solution.py:33
  388.2 11.0 %constant_dynamic-update-slice_fusion.30 = f32[27,16,1024]{2,1,0:T(8,128)S(1)} fusion(f32[16,1024]{1,0:T(8,128)S(1)} %multiply_add_fusion.26, f32[]{:T(128)} %bitcast.73, f32[]{:T(128)} %bitcast.72, f32[]{:T(128)} %bitcast.71, f32[]{:T(128)} %bitcast.70, f32[]{:T(128)} %bitcast.69, f32[]{:T(128)} %bitcast.68, f32[]{:T(128)} %bitcast.67, f32[]{:T(128)} %bitcast.66, ...), kind=kLoop, calls=%fused_computation.1476 | loop fusion | flops 540671 | bytes 131140
  399.2 10.8 %constant_dynamic-update-slice_fusion.29 = f32[27,16,1024]{2,1,0:T(8,128)S(1)} fusion(f32[27,16,1024]{2,1,0:T(8,128)S(1)} %constant_dynamic-update-slice_fusion.30, f32[16,1024]{1,0:T(8,128)S(1)} %multiply_add_fusion.25, f32[]{:T(128)} %bitcast.108, f32[]{:T(128)} %bitcast.107, f32[]{:T(128)} %bitcast.106, f32[]{:T(128)} %bitcast.105, f32[]{:T(128)} %bitcast.104, ...), kind=kLoop, calls=%fused_computation.1475 | loop fusion | flops 540672 | bytes 131140
  410.0 10.9 %constant_dynamic-update-slice_fusion.28 = f32[27,16,1024]{2,1,0:T(8,128)S(1)} fusion(f32[27,16,1024]{2,1,0:T(8,128)S(1)} %constant_dynamic-update-slice_fusion.29, f32[16,1024]{1,0:T(8,128)S(1)} %multiply_add_fusion.24, f32[]{:T(128)} %bitcast.143, f32[]{:T(128)} %bitcast.142, f32[]{:T(128)} %bitcast.141, f32[]{:T(128)} %bitcast.140, f32[]{:T(128)} %bitcast.139, ...), kind=kLoop, calls=%fused_computation.1474 | loop fusion | flops 540672 | bytes 131140
  420.9 11.1 %constant_dynamic-update-slice_fusion.27 = f32[27,16,1024]{2,1,0:T(8,128)S(1)} fusion(f32[27,16,1024]{2,1,0:T(8,128)S(1)} %constant_dynamic-update-slice_fusion.28, f32[16,1024]{1,0:T(8,128)S(1)} %multiply_add_fusion.23, f32[]{:T(128)} %bitcast.178, f32[]{:T(128)} %bitcast.177, f32[]{:T(128)} %bitcast.176, f32[]{:T(128)} %bitcast.175, f32[]{:T(128)} %bitcast.174, ...), kind=kLoop, calls=%fused_computation.1473 | loop fusion | flops 540672 | bytes 131140
  432.1 10.7 %constant_dynamic-update-slice_fusion.26 = f32[27,16,1024]{2,1,0:T(8,128)S(1)} fusion(f32[27,16,1024]{2,1,0:T(8,128)S(1)} %constant_dynamic-update-slice_fusion.27, f32[16,1024]{1,0:T(8,128)S(1)} %multiply_add_fusion.22, f32[]{:T(128)} %bitcast.213, f32[]{:T(128)} %bitcast.212, f32[]{:T(128)} %bitcast.211, f32[]{:T(128)} %bitcast.210, f32[]{:T(128)} %bitcast.209, ...), kind=kLoop, calls=%fused_computation.1472 | loop fusion | flops 540672 | bytes 131140
  442.8 10.9 %constant_dynamic-update-slice_fusion.25 = f32[27,16,1024]{2,1,0:T(8,128)S(1)} fusion(f32[27,16,1024]{2,1,0:T(8,128)S(1)} %constant_dynamic-update-slice_fusion.26, f32[16,1024]{1,0:T(8,128)S(1)} %multiply_add_fusion.21, f32[]{:T(128)} %bitcast.248, f32[]{:T(128)} %bitcast.247, f32[]{:T(128)} %bitcast.246, f32[]{:T(128)} %bitcast.245, f32[]{:T(128)} %bitcast.244, ...), kind=kLoop, calls=%fused_computation.1471 | loop fusion | flops 540672 | bytes 131140
  453.8 10.8 %constant_dynamic-update-slice_fusion.24 = f32[27,16,1024]{2,1,0:T(8,128)S(1)} fusion(f32[27,16,1024]{2,1,0:T(8,128)S(1)} %constant_dynamic-update-slice_fusion.25, f32[16,1024]{1,0:T(8,128)S(1)} %multiply_add_fusion.20, f32[]{:T(128)} %bitcast.283, f32[]{:T(128)} %bitcast.282, f32[]{:T(128)} %bitcast.281, f32[]{:T(128)} %bitcast.280, f32[]{:T(128)} %bitcast.279, ...), kind=kLoop, calls=%fused_computation.1470 | loop fusion | flops 540672 | bytes 131140
  464.5 10.8 %constant_dynamic-update-slice_fusion.23 = f32[27,16,1024]{2,1,0:T(8,128)S(1)} fusion(f32[27,16,1024]{2,1,0:T(8,128)S(1)} %constant_dynamic-update-slice_fusion.24, f32[16,1024]{1,0:T(8,128)S(1)} %multiply_add_fusion.19, f32[]{:T(128)} %bitcast.318, f32[]{:T(128)} %bitcast.317, f32[]{:T(128)} %bitcast.316, f32[]{:T(128)} %bitcast.315, f32[]{:T(128)} %bitcast.314, ...), kind=kLoop, calls=%fused_computation.1469 | loop fusion | flops 540672 | bytes 131140
  475.3 10.8 %constant_dynamic-update-slice_fusion.22 = f32[27,16,1024]{2,1,0:T(8,128)S(1)} fusion(f32[27,16,1024]{2,1,0:T(8,128)S(1)} %constant_dynamic-update-slice_fusion.23, f32[16,1024]{1,0:T(8,128)S(1)} %multiply_add_fusion.18, f32[]{:T(128)} %bitcast.353, f32[]{:T(128)} %bitcast.352, f32[]{:T(128)} %bitcast.351, f32[]{:T(128)} %bitcast.350, f32[]{:T(128)} %bitcast.349, ...), kind=kLoop, calls=%fused_computation.1468 | loop fusion | flops 540672 | bytes 131140
  486.2 10.9 %constant_dynamic-update-slice_fusion.21 = f32[27,16,1024]{2,1,0:T(8,128)S(1)} fusion(f32[27,16,1024]{2,1,0:T(8,128)S(1)} %constant_dynamic-update-slice_fusion.22, f32[16,1024]{1,0:T(8,128)S(1)} %multiply_add_fusion.17, f32[]{:T(128)} %bitcast.388, f32[]{:T(128)} %bitcast.387, f32[]{:T(128)} %bitcast.386, f32[]{:T(128)} %bitcast.385, f32[]{:T(128)} %bitcast.384, ...), kind=kLoop, calls=%fused_computation.1467 | loop fusion | flops 540672 | bytes 131140
  497.1 11.1 %constant_dynamic-update-slice_fusion.20 = f32[27,16,1024]{2,1,0:T(8,128)S(1)} fusion(f32[27,16,1024]{2,1,0:T(8,128)S(1)} %constant_dynamic-update-slice_fusion.21, f32[16,1024]{1,0:T(8,128)S(1)} %multiply_add_fusion.16, f32[]{:T(128)} %bitcast.423, f32[]{:T(128)} %bitcast.422, f32[]{:T(128)} %bitcast.421, f32[]{:T(128)} %bitcast.420, f32[]{:T(128)} %bitcast.419, ...), kind=kLoop, calls=%fused_computation.1466 | loop fusion | flops 540672 | bytes 131140
  508.1 10.9 %constant_dynamic-update-slice_fusion.19 = f32[27,16,1024]{2,1,0:T(8,128)S(1)} fusion(f32[27,16,1024]{2,1,0:T(8,128)S(1)} %constant_dynamic-update-slice_fusion.20, f32[16,1024]{1,0:T(8,128)S(1)} %multiply_add_fusion.15, f32[]{:T(128)} %bitcast.458, f32[]{:T(128)} %bitcast.457, f32[]{:T(128)} %bitcast.456, f32[]{:T(128)} %bitcast.455, f32[]{:T(128)} %bitcast.454, ...), kind=kLoop, calls=%fused_computation.1465 | loop fusion | flops 540672 | bytes 131140
  519.1 10.9 %constant_dynamic-update-slice_fusion.18 = f32[27,16,1024]{2,1,0:T(8,128)S(1)} fusion(f32[27,16,1024]{2,1,0:T(8,128)S(1)} %constant_dynamic-update-slice_fusion.19, f32[16,1024]{1,0:T(8,128)S(1)} %multiply_add_fusion.14, f32[]{:T(128)} %bitcast.493, f32[]{:T(128)} %bitcast.492, f32[]{:T(128)} %bitcast.491, f32[]{:T(128)} %bitcast.490, f32[]{:T(128)} %bitcast.489, ...), kind=kLoop, calls=%fused_computation.1464 | loop fusion | flops 540672 | bytes 131140
  530.0 11.0 %constant_dynamic-update-slice_fusion.17 = f32[27,16,1024]{2,1,0:T(8,128)S(1)} fusion(f32[27,16,1024]{2,1,0:T(8,128)S(1)} %constant_dynamic-update-slice_fusion.18, f32[16,1024]{1,0:T(8,128)S(1)} %multiply_add_fusion.13, f32[]{:T(128)} %bitcast.528, f32[]{:T(128)} %bitcast.527, f32[]{:T(128)} %bitcast.526, f32[]{:T(128)} %bitcast.525, f32[]{:T(128)} %bitcast.524, ...), kind=kLoop, calls=%fused_computation.1463 | loop fusion | flops 540672 | bytes 131140
  541.0 11.0 %constant_dynamic-update-slice_fusion.16 = f32[27,16,1024]{2,1,0:T(8,128)S(1)} fusion(f32[27,16,1024]{2,1,0:T(8,128)S(1)} %constant_dynamic-update-slice_fusion.17, f32[16,1024]{1,0:T(8,128)S(1)} %multiply_add_fusion.12, f32[]{:T(128)} %bitcast.563, f32[]{:T(128)} %bitcast.562, f32[]{:T(128)} %bitcast.561, f32[]{:T(128)} %bitcast.560, f32[]{:T(128)} %bitcast.559, ...), kind=kLoop, calls=%fused_computation.1462 | loop fusion | flops 540672 | bytes 131140
  552.0 10.7 %constant_dynamic-update-slice_fusion.15 = f32[27,16,1024]{2,1,0:T(8,128)S(1)} fusion(f32[27,16,1024]{2,1,0:T(8,128)S(1)} %constant_dynamic-update-slice_fusion.16, f32[16,1024]{1,0:T(8,128)S(1)} %multiply_add_fusion.11, f32[]{:T(128)} %bitcast.598, f32[]{:T(128)} %bitcast.597, f32[]{:T(128)} %bitcast.596, f32[]{:T(128)} %bitcast.595, f32[]{:T(128)} %bitcast.594, ...), kind=kLoop, calls=%fused_computation.1461 | loop fusion | flops 540672 | bytes 131140
  562.7 10.9 %constant_dynamic-update-slice_fusion.14 = f32[27,16,1024]{2,1,0:T(8,128)S(1)} fusion(f32[27,16,1024]{2,1,0:T(8,128)S(1)} %constant_dynamic-update-slice_fusion.15, f32[16,1024]{1,0:T(8,128)S(1)} %multiply_add_fusion.10, f32[]{:T(128)} %bitcast.633, f32[]{:T(128)} %bitcast.632, f32[]{:T(128)} %bitcast.631, f32[]{:T(128)} %bitcast.630, f32[]{:T(128)} %bitcast.629, ...), kind=kLoop, calls=%fused_computation.1460 | loop fusion | flops 540672 | bytes 131140
  573.6 10.9 %constant_dynamic-update-slice_fusion.13 = f32[27,16,1024]{2,1,0:T(8,128)S(1)} fusion(f32[27,16,1024]{2,1,0:T(8,128)S(1)} %constant_dynamic-update-slice_fusion.14, f32[16,1024]{1,0:T(8,128)S(1)} %multiply_add_fusion.9, f32[]{:T(128)} %bitcast.668, f32[]{:T(128)} %bitcast.667, f32[]{:T(128)} %bitcast.666, f32[]{:T(128)} %bitcast.665, f32[]{:T(128)} %bitcast.664, ...), kind=kLoop, calls=%fused_computation.1459 | loop fusion | flops 540672 | bytes 131140
  584.5 11.1 %constant_dynamic-update-slice_fusion.12 = f32[27,16,1024]{2,1,0:T(8,128)S(1)} fusion(f32[27,16,1024]{2,1,0:T(8,128)S(1)} %constant_dynamic-update-slice_fusion.13, f32[16,1024]{1,0:T(8,128)S(1)} %multiply_add_fusion.8, f32[]{:T(128)} %bitcast.703, f32[]{:T(128)} %bitcast.702, f32[]{:T(128)} %bitcast.701, f32[]{:T(128)} %bitcast.700, f32[]{:T(128)} %bitcast.699, ...), kind=kLoop, calls=%fused_computation.1458 | loop fusion | flops 540672 | bytes 131140
  595.7 10.9 %constant_dynamic-update-slice_fusion.11 = f32[27,16,1024]{2,1,0:T(8,128)S(1)} fusion(f32[27,16,1024]{2,1,0:T(8,128)S(1)} %constant_dynamic-update-slice_fusion.12, f32[16,1024]{1,0:T(8,128)S(1)} %multiply_add_fusion.7, f32[]{:T(128)} %bitcast.738, f32[]{:T(128)} %bitcast.737, f32[]{:T(128)} %bitcast.736, f32[]{:T(128)} %bitcast.735, f32[]{:T(128)} %bitcast.734, ...), kind=kLoop, calls=%fused_computation.1457 | loop fusion | flops 540672 | bytes 131140
  606.5 11.2 %constant_dynamic-update-slice_fusion.10 = f32[27,16,1024]{2,1,0:T(8,128)S(1)} fusion(f32[27,16,1024]{2,1,0:T(8,128)S(1)} %constant_dynamic-update-slice_fusion.11, f32[16,1024]{1,0:T(8,128)S(1)} %multiply_add_fusion.6, f32[]{:T(128)} %bitcast.773, f32[]{:T(128)} %bitcast.772, f32[]{:T(128)} %bitcast.771, f32[]{:T(128)} %bitcast.770, f32[]{:T(128)} %bitcast.769, ...), kind=kLoop, calls=%fused_computation.1456 | loop fusion | flops 540672 | bytes 131140
  617.7 11.0 %constant_dynamic-update-slice_fusion.9 = f32[27,16,1024]{2,1,0:T(8,128)S(1)} fusion(f32[27,16,1024]{2,1,0:T(8,128)S(1)} %constant_dynamic-update-slice_fusion.10, f32[16,1024]{1,0:T(8,128)S(1)} %multiply_add_fusion.5, f32[]{:T(128)} %bitcast.808, f32[]{:T(128)} %bitcast.807, f32[]{:T(128)} %bitcast.806, f32[]{:T(128)} %bitcast.805, f32[]{:T(128)} %bitcast.804, ...), kind=kLoop, calls=%fused_computation.1455 | loop fusion | flops 540672 | bytes 131140
  628.8 11.0 %constant_dynamic-update-slice_fusion.8 = f32[27,16,1024]{2,1,0:T(8,128)S(1)} fusion(f32[27,16,1024]{2,1,0:T(8,128)S(1)} %constant_dynamic-update-slice_fusion.9, f32[16,1024]{1,0:T(8,128)S(1)} %multiply_add_fusion.4, f32[]{:T(128)} %bitcast.843, f32[]{:T(128)} %bitcast.842, f32[]{:T(128)} %bitcast.841, f32[]{:T(128)} %bitcast.840, f32[]{:T(128)} %bitcast.839, ...), kind=kLoop, calls=%fused_computation.1454 | loop fusion | flops 540672 | bytes 131140
  639.7 11.1 %constant_dynamic-update-slice_fusion.7 = f32[27,16,1024]{2,1,0:T(8,128)S(1)} fusion(f32[27,16,1024]{2,1,0:T(8,128)S(1)} %constant_dynamic-update-slice_fusion.8, f32[16,1024]{1,0:T(8,128)S(1)} %multiply_add_fusion.3, f32[]{:T(128)} %bitcast.878, f32[]{:T(128)} %bitcast.877, f32[]{:T(128)} %bitcast.876, f32[]{:T(128)} %bitcast.875, f32[]{:T(128)} %bitcast.874, ...), kind=kLoop, calls=%fused_computation.1453 | loop fusion | flops 540672 | bytes 131140
  650.8 10.6 %constant_dynamic-update-slice_fusion.6 = f32[27,16,1024]{2,1,0:T(8,128)S(1)} fusion(f32[27,16,1024]{2,1,0:T(8,128)S(1)} %constant_dynamic-update-slice_fusion.7, f32[16,1024]{1,0:T(8,128)S(1)} %multiply_add_fusion.2, f32[]{:T(128)} %bitcast.913, f32[]{:T(128)} %bitcast.912, f32[]{:T(128)} %bitcast.911, f32[]{:T(128)} %bitcast.910, f32[]{:T(128)} %bitcast.909, ...), kind=kLoop, calls=%fused_computation.1452 | loop fusion | flops 540672 | bytes 131140
  661.4 10.8 %constant_dynamic-update-slice_fusion.5 = f32[27,16,1024]{2,1,0:T(8,128)S(1)} fusion(f32[27,16,1024]{2,1,0:T(8,128)S(1)} %constant_dynamic-update-slice_fusion.6, f32[16,1024]{1,0:T(8,128)S(1)} %multiply_add_fusion.1, f32[]{:T(128)} %bitcast.948, f32[]{:T(128)} %bitcast.947, f32[]{:T(128)} %bitcast.946, f32[]{:T(128)} %bitcast.945, f32[]{:T(128)} %bitcast.944, ...), kind=kLoop, calls=%fused_computation.1451 | loop fusion | flops 540672 | bytes 131140
  672.3 10.9 %constant_dynamic-update-slice_fusion.4 = f32[27,16,1024]{2,1,0:T(8,128)S(1)} fusion(f32[27,16,1024]{2,1,0:T(8,128)S(1)} %constant_dynamic-update-slice_fusion.5, f32[16,1024]{1,0:T(8,128)S(1)} %multiply_add_fusion, f32[]{:T(128)} %bitcast.983, f32[]{:T(128)} %bitcast.982, f32[]{:T(128)} %bitcast.981, f32[]{:T(128)} %bitcast.980, f32[]{:T(128)} %bitcast.979, ...), kind=kLoop, calls=%fused_computation.1450 | loop fusion | flops 540672 | bytes 131140 | tf_op jit(solution)/shard_map/stack | solution.py:67
  738.9 94.1 %all-gather.4.cloned.1.call-done = f32[27,128,1024]{2,1,0:T(8,128)} async-done(((f32[27,16,1024]{2,1,0:T(8,128)}), f32[27,128,1024]{2,1,0:T(8,128)}) %all-gather.4.cloned.1.call-update) | async-done | bytes 14155792 | tf_op jit(solution)/shard_map/all_gather | solution.py:75
  841.0 8.1 collective-permute-start.3
  850.3 6.2 fusion.28
  856.5 7.5 fusion.17
  864.0 44.1 %all-gather.6.cloned.1.call-done = bf16[1024,1024]{1,0:T(8,128)(2,1)} async-done(((bf16[128,1024]{1,0:T(8,128)(2,1)}), bf16[1024,1024]{1,0:T(8,128)(2,1)}) %all-gather.6.cloned.1.call-update) | async-done | bytes 2097168 | tf_op jit(solution)/shard_map/all_gather | solution.py:97
  911.2 7.9 collective-permute-start.5
  922.4 17.7 %psum.7 = f32[]{:T(128)} all-reduce(f32[]{:T(128)S(6)} %mul.8618), channel_id=1, replica_groups=mesh['sky'=64,'epoch'=8] {'epoch'}, use_global_device_ids=true, to_apply=%region_2.3 | all-reduce | flops 1 | bytes 8 | tf_op jit(solution)/shard_map/psum | solution.py:93
  944.8 67.6 %while.13 = (s32[]{:T(128)}, f32[128,1024]{1,0:T(8,128)S(1)}, s32[]{:T(128)}, bf16[8,160,1056]{2,1,0:T(8,128)(2,1)S(1)}, s32[]{:T(128)}, /*index=5*/s32[24,8,2]{...) while((s32[]{:T(128)}, f32[128,1024]{1,0:T(8,128)S(1)}, ...), condition=%wide.region_4.5_spmd, body=%wide.region_3.4_spmd.sunk | while | flops 2228295 | bytes 8553703 | solution.py:109
  1012.8 11.0 %all_to_all.12 = f32[1,128,1024]{2,0,1:T(1,128)S(1)} all-to-all(f32[1,128,1024]{2,0,1:T(1,128)S(1)} %broadcast_in_dim.13), channel_id=1, replica_groups=mesh['sky'=64,'epoch'=8] {'epoch'}, dimensions={1} | all-to-all | bytes 1048576 | tf_op jit(solution)/shard_map/all_to_all | solution.py:112
  (138 shorter events, 130.9 us)
Async XLA Ops:
  6.5 103.0 %copy-start = (f32[16,1024]{1,0:T(8,128)S(1)}, f32[16,1024]{1,0:T(8,128)}, u32[]{:S(2)}) copy-start(f32[16,1024]{1,0:T(8,128)} %param.11) | copy-start | bytes 196612
  6.5 826.4 %all-gather.4.cloned.1.call-start = ((), (), s32[]{:S(2)}) async-start(), calls=%async_computation.1 | async-start | bytes 15925248 | tf_op jit(solution)/shard_map/all_gather | solution.py:75
  7.4 90.0 %collective-permute-start = (f32[8,1024]{1,0:T(8,128)S(1)}, f32[8,1024]{1,0:T(8,128)S(1)}, u32[]{:S(2)}, u32[]{:S(2)}) collective-permute-start(f32[8,1024]{1,0:T(8,128)S(1)} %get-tuple-element.181), channel_id=1, source_target_pairs={{0,1},{1,2},{2,3},{3,4},{4,5},{5,6},{6,7},{7,8},{8,9},{9,10},{10,1... | collective-permute-start | bytes 98312 | tf_op jit(solution)/shard_map/ppermute | solution.py:20
  10.8 87.5 %collective-permute-start.1 = (f32[8,1024]{1,0:T(8,128)S(1)}, f32[8,1024]{1,0:T(8,128)S(1)}, u32[]{:S(2)}, u32[]{:S(2)}) collective-permute-start(f32[8,1024]{1,0:T(8,128)S(1)} %get-tuple-element.182), channel_id=1, source_target_pairs={{1,0},{2,1},{3,2},{4,3},{5,4},{6,5},{7,6},{8,7},{9,8},{10,9},{11,1... | collective-permute-start | bytes 98312 | tf_op jit(solution)/shard_map/ppermute | solution.py:22
  584.5 99.9 %copy-start.3 = (f32[1,1,27,3]{2,1,3,0:T(1,128)S(1)}, f32[1,1,27,3]{2,1,3,0:T(1,128)}, u32[]{:S(2)}) copy-start(f32[1,1,27,3]{2,1,3,0:T(1,128)} %param.13) | copy-start | bytes 976
  628.7 204.2 %copy-start.4 = (f32[1,128,1024]{2,1,0:T(8,128)S(1)}, f32[1,128,1024]{2,1,0:T(8,128)}, u32[]{:S(2)}) copy-start(f32[1,128,1024]{2,1,0:T(8,128)} %param.10) | copy-start | bytes 1572868
  683.2 1.2 copy-start.2
  684.4 223.8 %all-gather.6.cloned.1.call-start = ((), (), s32[]{:S(2)}) async-start(), calls=%async_computation.2 | async-start | bytes 2359296 | tf_op jit(solution)/shard_map/all_gather | solution.py:97
  833.0 16.1 %copy-start.5 = (f32[1,9]{1,0:T(1,128)S(1)}, f32[1,9]{1,0:T(1,128)}, u32[]{:S(2)}) copy-start(f32[1,9]{1,0:T(1,128)} %param.14) | copy-start | bytes 112
  833.0 23.5 %copy-start.1 = (f32[1,128,1024]{2,1,0:T(8,128)S(1)}, f32[1,128,1024]{2,1,0:T(8,128)}, u32[]{:S(2)}) copy-start(f32[1,128,1024]{2,1,0:T(8,128)} %param.15) | copy-start | bytes 1572868
  839.0 10.7 %collective-permute-start.2 = (f32[4,1024]{1,0:T(4,128)S(1)}, f32[4,1024]{1,0:T(4,128)S(1)}, u32[]{:S(2)}, u32[]{:S(2)}) collective-permute-start(f32[4,1024]{1,0:T(4,128)S(1)} %get-tuple-element.177), channel_id=1, source_target_pairs={{0,8},{8,16},{16,24},{24,32},{32,40},{40,48},{48,56},{56,64},{64,7... | collective-permute-start | bytes 49160 | tf_op jit(solution)/shard_map/ppermute | solution.py:20
  841.0 9.3 collective-permute-start.3
  856.5 84.3 %copy-start.6 = (s32[1,24,8,2]{1,3,2,0:T(2,128)S(1)}, s32[1,24,8,2]{1,3,2,0:T(2,128)}, u32[]{:S(2)}) copy-start(s32[1,24,8,2]{1,3,2,0:T(2,128)} %param.16) | copy-start | bytes 4612
  909.2 32.4 %collective-permute-start.4 = (bf16[8,16,1024]{2,1,0:T(8,128)(2,1)S(1)}, bf16[8,16,1024]{2,1,0:T(8,128)(2,1)S(1)}, u32[]{:S(2)}, u32[]{:S(2)}) collective-permute-start(bf16[8,16,1024]{2,1,0:T(8,128)(2,1)S(1)} %get-tuple-element.175), channel_id=1, source_target_pairs={{0,8},{8,16},{16,24},{24,32},{32,40},{40,48},{48,56},{56,64},{64,7... | collective-permute-start | bytes 786440 | tf_op jit(solution)/shard_map/ppermute | solution.py:20
  911.2 30.4 %collective-permute-start.5 = (bf16[8,16,1024]{2,1,0:T(8,128)(2,1)S(1)}, bf16[8,16,1024]{2,1,0:T(8,128)(2,1)S(1)}, u32[]{:S(2)}, u32[]{:S(2)}) collective-permute-start(bf16[8,16,1024]{2,1,0:T(8,128)(2,1)S(1)} %get-tuple-element.176), channel_id=1, source_target_pairs={{8,0},{16,8},{24,16},{32,24},{40,32},{48,40},{56,48},{64,56},{72,6... | collective-permute-start | bytes 786440 | tf_op jit(solution)/shard_map/ppermute | solution.py:22
Sparse Core Ops, SparseCore 0:
  684.5 148.4 all-gather.3
  864.2 43.9 all-gather.5
where the time goes:
time: 1040 us; the launch traced here: 1030 us
  other arithmetic  631 us (61%)
  waiting for transfers between devices  139 us (13%)
  local copies, waits for them, and re-layouts  90.4 us (9%)
  loops' own time  60.3 us (6%)
  between operations  51.3 us (5%)
  starting transfers between devices  30.8 us (3%)
  blocking collectives  28.7 us (3%)
    add x28, other arithmetic, conv_rows(): result = result + kernel[offset] * extended[offset:offset + height]  296 us
    unnamed x26, other arithmetic  284 us
    all_gather x1, waiting for transfers between devices, on_device(): gathered_maps = lax.all_gather(band_maps, 'epoch', axis=1, tiled=True)  94.1 us
    another operation x1, loops' own time, on_device(): lax.fori_loop(0, own_turns, visit_own, jnp.full((height, columns), -1e+30...  60.3 us
    all_gather x1, waiting for transfers between devices, on_device(): every_epoch = lax.all_gather(filtered[None], 'epoch', axis=0, tiled=True)  44.1 us
    slice x27, local copies, waits for them, and re-layouts, conv_cols(): result = kernel[0] * padded[:, 0:columns]  41.8 us
    slice x18, local copies, waits for them, and re-layouts, conv_rows(): result = kernel[0] * extended[0:height]  28.3 us
    ppermute x3, starting transfers between devices, padded_2(): lax.ppermute(head, axis, [((i + 1) % count, i) for i in range(ends)])  23.5 us
  transfers between devices with their start and end apart: 8, of which 3 were waited for; matrix products, arithmetic and copies ran while one was open for 10% of the time, Pallas kernels for 0%

commit v1 on v0

v1 whole, which is shorter than its diff:
```python
import jax
import jax.numpy as jnp
from jax import lax
from jax.experimental import pallas as pl
from jax.experimental.pallas import tpu as pltpu
from jax.sharding import PartitionSpec as P

NB = 27
R = 8
F = 4
SMAX = 16
EPOCHS = 8
H = 128
W = 1024
BAND = 16
TAPS = 2 * R + 1
PTAPS = 2 * F + 1
VEDGE = 24
TEDGE = 32
MID = 56
MWIN = 80
EDGE = 32
EWIN = 48
NBLK = 256
PADW = W + 128
OUTR = 56
DROWS = 2 * EDGE + 2 * MID
FROWS = H + 2 * SMAX
MIDDLE = (H - 1) / 2.0
f32 = jnp.float32
bf16 = jnp.bfloat16


def toeplitz(coeff_rows, col_taps, row_taps, table):
    scaled = [col_taps * rows[p:p + 1, :] for rows in coeff_rows for p in range(3)]
    profiles = jnp.dot(jnp.concatenate(scaled, axis=0), row_taps,
                       precision=lax.Precision.HIGHEST, preferred_element_type=f32)
    for s in range(8):
        moved = profiles if s == 0 else pltpu.roll(profiles, s, 1)
        for i in range(len(scaled)):
            table[i, pl.ds(s, 24, stride=8), :] = moved[24 * i:24 * i + 24]


def band_rows(table, at, window, offset, first_row, lanes, store):
    lane = lax.broadcasted_iota(jnp.int32, (8, 128), 1)
    row = lax.broadcasted_iota(jnp.int32, (8, 128), 0) + first_row
    w = (row.astype(f32) - MIDDLE) / MIDDLE
    for q in range((lanes + 127) // 128):
        even, odd = jnp.zeros((8, 128), f32), jnp.zeros((8, 128), f32)
        for l in range(TAPS):
            a = l * window + offset
            low = a % 128
            if a // 128 == q:
                keep = None if low + 24 <= 128 else lane >= low
            elif (a + 23) // 128 == q:
                keep = lane < 24
            else:
                continue
            parts = []
            for p in range(3):
                piece = table[at + p, 8 * l:8 * l + 8, :]
                if low:
                    piece = pltpu.roll(piece, low, 1)
                if keep is not None:
                    piece = jnp.where(keep, piece, 0.0)
                parts.append(piece)
            even = even + (parts[0] + w * parts[2])
            odd = odd + parts[1]
        store(q, even, odd)


def split(x):
    hi = x.astype(bf16)
    return hi, (x - hi.astype(f32)).astype(bf16)


def shift_band(band, hi_ref, lo_ref, at):
    blank = jnp.zeros((BAND, PADW - W), bf16)
    for piece, ref in zip(split(band), (hi_ref, lo_ref)):
        piece = jnp.concatenate([piece, blank], axis=1)
        for l in range(TAPS):
            moved = piece if l == R else pltpu.roll(piece, (R - l) % PADW, 1)
            ref[l, at:at + BAND, :] = moved[:, 0:W]


def model_block(lhs, hi_ref, lo_ref, rows, count, n):
    cols = slice(n * NBLK, (n + 1) * NBLK)
    depth = TAPS * (rows.stop - rows.start)
    acc = jnp.dot(lhs, hi_ref[:, rows, cols].reshape(depth, NBLK), preferred_element_type=f32)
    acc = acc[0:2 * count] + acc[2 * count:4 * count] + jnp.dot(
        lhs[0:2 * count], lo_ref[:, rows, cols].reshape(depth, NBLK), preferred_element_type=f32)
    col = lax.broadcasted_iota(jnp.int32, (count, NBLK), 1) + n * NBLK
    u = (col.astype(f32) - (W - 1) / 2.0) / ((W - 1) / 2.0)
    return acc[0:count] + u * acc[count:2 * count]


def row_filter(psf, lhs, wide):
    lane = lax.broadcasted_iota(jnp.int32, (8, 128), 1)
    sub = lax.broadcasted_iota(jnp.int32, (8, 128), 0)
    taps = jnp.zeros((8, 128), f32)
    for k in range(PTAPS):
        taps = jnp.where(lane - sub == k, psf[k], taps)
    for g in range(FROWS // 8):
        low = (8 * g + 4) % 128
        moved = pltpu.roll(taps, low, 1)
        first, second = (8 * g + 4) // 128, (8 * g + 19) // 128
        pieces = [jnp.zeros((8, 128), f32)] * 2
        if first == second:
            pieces[first] = moved
        else:
            pieces[first] = jnp.where(lane >= low, moved, 0.0)
            pieces[second] = jnp.where(lane < low, moved, 0.0)
        wide[8 * g:8 * g + 8, 0:128] = pieces[0]
        wide[8 * g:8 * g + 8, 128:DROWS] = pieces[1][:, 0:DROWS - 128]
    hi, lo = split(wide[...])
    lhs[0:FROWS, :] = hi
    lhs[FROWS:2 * FROWS, :] = lo


def prepare_kernel(psf, inv_var, coeffs, col_taps, row_taps, lhs, weight, smoother, table, wide, psf_wide):
    row_filter(psf, smoother, psf_wide)
    toeplitz([coeffs[...]], col_taps[...], row_taps[...], table)
    lanes = TAPS * MWIN
    for block in range(2):
        for g in range(MID // 8):
            def store(q, even, odd, block=block, g=g):
                end = min(128, lanes - q * 128)
                wide[block, 8 * g:8 * g + 8, q * 128:q * 128 + end] = even[:, 0:end]
                wide[block, MID + 8 * g:MID + 8 * g + 8, q * 128:q * 128 + end] = odd[:, 0:end]
            band_rows(table, 0, MWIN, 8 * g + 8 * block, 8 + MID * block + 8 * g, lanes, store)
        hi, lo = split(wide[block])
        lhs[block, 0:2 * MID, :] = hi
        lhs[block, 2 * MID:4 * MID, :] = lo
    power = psf[0] * psf[0]
    for k in range(1, PTAPS):
        power = power + psf[k] * psf[k]
    weight[...] = jnp.full((8, 128), power * power * (jnp.sum(inv_var[...]) / (H * W)), f32)


def inner_kernel(bands, lhs, visits, diff, hi_ref, lo_ref):
    for e in range(EPOCHS):
        shift_band(bands[e], hi_ref, lo_ref, e * BAND)
    for block in range(2):
        rows = slice(0, MWIN) if block == 0 else slice(H - MWIN, H)
        for n in range(W // NBLK):
            cols = slice(n * NBLK, (n + 1) * NBLK)
            model = model_block(lhs[block], hi_ref, lo_ref, rows, MID, n)
            diff[MID * block:MID * (block + 1), cols] = visits[8 + MID * block:8 + MID * (block + 1), cols] - model


def outer_kernel(psf, visits, inv_var, above, below, bands, inner, coeffs, col_taps, row_taps, weight, smoother,
                 out, table, wide, lhs, hi_ref, lo_ref, diff, smoothed):
    toeplitz([above[40:48, 0:128], coeffs[...], below[40:48, 0:128]], col_taps[...], row_taps[...], table)
    lanes = TAPS * EWIN
    for block in range(2):
        for g in range(4):
            if block == 0:
                at, first = (0, H - VEDGE + 8 * g) if g < 3 else (3, 0)
            else:
                at, first = (6, 8 * (g - 1)) if g > 0 else (3, H - 8)

            def store(q, even, odd, block=block, g=g):
                end = min(128, lanes - q * 128)
                wide[block, 8 * g:8 * g + 8, q * 128:q * 128 + end] = even[:, 0:end]
                wide[block, EDGE + 8 * g:EDGE + 8 * g + 8, q * 128:q * 128 + end] = odd[:, 0:end]
            band_rows(table, at, EWIN, 8 * g, first, lanes, store)
        hi, lo = split(wide[block])
        lhs[block, 0:2 * EDGE, :] = hi
        lhs[block, 2 * EDGE:4 * EDGE, :] = lo
    shift_band(above[48:64, :], hi_ref, lo_ref, 0)
    shift_band(above[64:80, :], hi_ref, lo_ref, 16)
    shift_band(bands[0], hi_ref, lo_ref, 32)
    shift_band(bands[EPOCHS - 1], hi_ref, lo_ref, 48)
    shift_band(below[48:64, :], hi_ref, lo_ref, 64)
    shift_band(below[64:80, :], hi_ref, lo_ref, 80)
    diff[EDGE:EDGE + 2 * MID, :] = inner[...]
    low = EDGE + 2 * MID
    for n in range(W // NBLK):
        cols = slice(n * NBLK, (n + 1) * NBLK)
        model = model_block(lhs[0], hi_ref, lo_ref, slice(0, EWIN), EDGE, n)
        diff[0:VEDGE, cols] = above[0:VEDGE, cols] - model[0:VEDGE]
        diff[VEDGE:EDGE, cols] = visits[0:8, cols] - model[VEDGE:EDGE]
        model = model_block(lhs[1], hi_ref, lo_ref, slice(EWIN, 2 * EWIN), EDGE, n)
        diff[low:low + 8, cols] = visits[H - 8:H, cols] - model[0:8]
        diff[low + 8:low + EDGE, cols] = below[0:VEDGE, cols] - model[8:EDGE]

    smoothed[:, W:PADW] = jnp.zeros((FROWS, PADW - W), f32)
    for n in range(W // NBLK):
        cols = slice(n * NBLK, (n + 1) * NBLK)
        hi, lo = split(diff[:, cols])
        both = jnp.dot(smoother[...], hi, preferred_element_type=f32)
        smoothed[:, cols] = both[0:FROWS] + both[FROWS:2 * FROWS] + jnp.dot(
            smoother[0:FROWS, :], lo, preferred_element_type=f32)
    for c in range(10):
        smooth = smoothed[16 * c:16 * c + 16, :]
        total = psf[F] * smooth
        for k in range(PTAPS):
            if k != F:
                total = total + psf[k] * pltpu.roll(smooth, (F - k) % PADW, 1)
        total = total[:, 0:W]
        if c == 0:
            scale = above[24:40, :]
        elif c == 9:
            scale = below[24:40, :]
        else:
            scale = inv_var[16 * (c - 1):16 * c, :]
        rounded = (total * scale).astype(bf16)
        for part in range(3):
            owner = c - part
            if 0 <= owner < EPOCHS:
                out[owner, part * 16:(part + 1) * 16, :] = rounded
    first = weight[...].astype(bf16)
    rest = weight[...] - first.astype(f32)
    second = rest.astype(bf16)
    third = (rest - second.astype(f32)).astype(bf16)
    last = jnp.concatenate([first, second, third, jnp.zeros((8, W - 384), bf16)], axis=1)
    for owner in range(EPOCHS):
        out[owner, 48:OUTR, :] = last


def search_kernel(count, shifts, windows, out, table):
    weight_sum = jnp.zeros((8, 128), f32)
    for e in range(EPOCHS):
        rows = windows[e, 0:48, :].astype(f32)
        for q in range(8):
            table[e, pl.ds(q, 48, stride=8), :] = rows[:, q * 128:(q + 1) * 128]
        for q in range(3):
            weight_sum = weight_sum + windows[e, 48:OUTR, q * 128:(q + 1) * 128].astype(f32)
    lane = lax.broadcasted_iota(jnp.int32, (8, 128), 1)
    sub = lax.broadcasted_iota(jnp.int32, (8, 128), 0)
    right = (lane >= 64)[None]
    from_next = ((lane >= 64) & (sub < 7))[None]
    from_last = ((lane < 64) & (sub > 0))[None]

    def stack(v, half):
        whole = jnp.zeros((8, 8, 128), f32)
        inside = jnp.zeros((8, 8, 128), f32)
        for e in range(EPOCHS):
            down = shifts[v * 16 + 2 * e]
            across = shifts[v * 16 + 2 * e + 1]
            first = pl.multiple_of((SMAX + 8 * half + down) * 8, 8)
            window = table[e, pl.ds(first, 64), :]
            moved = pltpu.roll(window, (128 - across) % 128, 1).reshape(8, 8, 128)
            source = lane + across
            keep = ((source >= 0) & (source < 128))[None]
            whole = whole + moved
            inside = inside + jnp.where(keep, moved, 0.0)
        outside = whole - inside
        total = inside + jnp.where(from_next, pltpu.roll(outside, 7, 1), 0.0)
        return total + jnp.where(from_last, pltpu.roll(outside, 1, 1), 0.0)

    most = count[0] - 1

    def step(turn, best):
        first, second = 2 * turn, jnp.minimum(2 * turn + 1, most)
        tops = jnp.maximum(best[0], jnp.maximum(stack(first, 0), stack(second, 0)))
        lows = jnp.maximum(best[1], jnp.maximum(stack(first, 1), stack(second, 1)))
        return tops, lows

    least = jnp.full((8, 8, 128), -1e30, f32)
    best = lax.fori_loop(0, (count[0] + 1) // 2, step, (least, least))
    norm = jnp.sqrt(weight_sum)[None]
    for half in range(2):
        table[0, half * 64:half * 64 + 64, :] = (best[half] / norm).reshape(64, 128)
    for q in range(8):
        out[:, q * 128:(q + 1) * 128] = table[0, pl.ds(q, BAND, stride=8), :]


def vmem(count):
    return [pl.BlockSpec(memory_space=pltpu.VMEM)] * count


def smem(count):
    return [pl.BlockSpec(memory_space=pltpu.SMEM)] * count


def shape(*dims, dtype=f32):
    return jax.ShapeDtypeStruct(dims, dtype)


def held(x):
    return pltpu.with_memory_space_constraint(x, pltpu.VMEM)


def on_device(visits, template, basis_taps, coeffs, psf_taps, inv_var, shifts, vel_count):
    visits, inv_var, psf = visits[0], inv_var[0], psf_taps[0]
    tiles = lax.axis_size("sky")
    epochs = lax.axis_size("epoch")
    bands = lax.all_to_all(jnp.broadcast_to(template[None], (epochs, BAND, W)), "epoch", 0, 0, tiled=True)
    own = jnp.pad(coeffs[0, 0].T, ((0, 5), (0, 128 - NB)))
    wide = jnp.pad(own, ((0, 0), (0, W - 128)))
    col_taps = jnp.pad(basis_taps[1].T, ((0, 24 - TAPS), (0, 128 - NB)))
    row_taps = jnp.pad(basis_taps[0], ((0, 128 - NB), (0, 128 - TAPS)))
    lhs, weight, smoother = pl.pallas_call(
        prepare_kernel,
        out_shape=(
            pltpu.VMEM((2, 4 * MID, TAPS * MWIN), bf16),
            shape(8, 128),
            pltpu.VMEM((2 * FROWS, DROWS), bf16),
        ),
        in_specs=smem(1) + vmem(4),
        out_specs=tuple(vmem(3)),
        scratch_shapes=[
            pltpu.VMEM((3, 192, 128), f32),
            pltpu.VMEM((2, 2 * MID, TAPS * MWIN), f32),
            pltpu.VMEM((FROWS, DROWS), f32),
        ],
        compiler_params=pltpu.CompilerParams(vmem_limit_bytes=8 << 20),
        name="prepare",
    )(psf, held(inv_var), held(own), held(col_taps), held(row_taps))
    bands, weight = lax.optimization_barrier((bands, weight))
    to_below = jnp.concatenate([visits[H - VEDGE:], inv_var[H - SMAX:], wide, bands[6:].reshape(TEDGE, W)], axis=0)
    to_above = jnp.concatenate([visits[:VEDGE], inv_var[:SMAX], wide, bands[:2].reshape(TEDGE, W)], axis=0)
    above = lax.ppermute(to_below, "sky", [(i, i + 1) for i in range(tiles - 1)])
    below = lax.ppermute(to_above, "sky", [(i + 1, i) for i in range(tiles - 1)])
    inner = pl.pallas_call(
        inner_kernel,
        out_shape=pltpu.VMEM((2 * MID, W), f32),
        in_specs=vmem(3),
        out_specs=vmem(1)[0],
        scratch_shapes=[pltpu.VMEM((TAPS, H, W), bf16), pltpu.VMEM((TAPS, H, W), bf16)],
        compiler_params=pltpu.CompilerParams(vmem_limit_bytes=24 << 20),
        name="inner",
    )(held(bands), lhs, held(visits))
    windows = pl.pallas_call(
        outer_kernel,
        out_shape=shape(EPOCHS, OUTR, W, dtype=bf16),
        in_specs=smem(1) + vmem(11),
        out_specs=vmem(1)[0],
        scratch_shapes=[
            pltpu.VMEM((9, 192, 128), f32),
            pltpu.VMEM((2, 2 * EDGE, TAPS * EWIN), f32),
            pltpu.VMEM((2, 4 * EDGE, TAPS * EWIN), bf16),
            pltpu.VMEM((TAPS, 2 * EWIN, W), bf16),
            pltpu.VMEM((TAPS, 2 * EWIN, W), bf16),
            pltpu.VMEM((DROWS, W), f32),
            pltpu.VMEM((FROWS, PADW), f32),
        ],
        compiler_params=pltpu.CompilerParams(vmem_limit_bytes=24 << 20),
        name="outer",
    )(psf, held(visits), held(inv_var), held(above), held(below), held(bands), inner, held(own), held(col_taps), held(row_taps),
      held(weight), smoother)
    moved = lax.all_to_all(windows, "epoch", 0, 0, tiled=True)
    return pl.pallas_call(
        search_kernel,
        out_shape=shape(BAND, W),
        in_specs=smem(2) + vmem(1),
        out_specs=vmem(1)[0],
        scratch_shapes=[pltpu.VMEM((EPOCHS, 384, 128), f32)],
        compiler_params=pltpu.CompilerParams(vmem_limit_bytes=8 << 20),
        name="search",
    )(vel_count, shifts.reshape(-1), held(moved))


def solution(mesh):
    in_specs = (
        P("epoch", "sky", None),
        P(("sky", "epoch"), None),
        P(),
        P("epoch", "sky", None, None),
        P("epoch", None),
        P("epoch", "sky", None),
        P("sky", None, None, None),
        P("sky"),
    )
    out_specs = P(("sky", "epoch"), None)
    return jax.shard_map(
        on_device, mesh=mesh, in_specs=in_specs, out_specs=out_specs, check_vma=False
    )
```

time: 1040 us -> 62.1 us (0.06)
  the two profiles are of different devices: /device:TPU:256 before, /device:TPU:249 now
where the time goes in v1:
time: 62.1 us
  waiting for transfers between devices  22.6 us (36%)
  starting transfers between devices  18.9 us (30%)
  Pallas kernels  17.5 us (28%)
  local copies, waits for them, and re-layouts  2.24 us (4%)
  between operations  0.8 us (1%)
    all_to_all x1, waiting for transfers between devices, on_device(): moved = lax.all_to_all(windows, 'epoch', 0, 0, tiled=True)  12.4 us
    all_to_all x1, waiting for transfers between devices, on_device(): lax.all_to_all(jnp.broadcast_to(template[None], (epochs, BAND, W)), 'epoc...  7.09 us
    ppermute x1, starting transfers between devices, on_device(): lax.ppermute(to_below, 'sky', [(i, i + 1) for i in range(tiles - 1)])  7.08 us
    pallas_call x1, Pallas kernels, on_device(): pl.pallas_call(outer_kernel, out_shape=shape(EPOCHS, OUTR, W, dtype=bf16)...  6.98 us
    pallas_call x1, Pallas kernels, on_device(): pl.pallas_call(search_kernel, out_shape=shape(BAND, W), in_specs=smem(2)...  5.84 us
    all_to_all x1, starting transfers between devices, on_device(): lax.all_to_all(jnp.broadcast_to(template[None], (epochs, BAND, W)), 'epoc...  5.2 us
    all_to_all x1, starting transfers between devices, on_device(): moved = lax.all_to_all(windows, 'epoch', 0, 0, tiled=True)  3.9 us
    ppermute x1, waiting for transfers between devices, on_device(): lax.ppermute(to_above, 'sky', [(i + 1, i) for i in range(tiles - 1)])  3.13 us
  transfers between devices with their start and end apart: 4, of which 3 were waited for; matrix products, arithmetic and copies ran while one was open for 1% of the time, Pallas kernels for 8%

profile of v1, /device:TPU:249, one launch (start us, length us, event | category | flops | bytes accessed | tf_op | source)
XLA Modules:
  0.0 62.1 jit_solution(7589076612623041967)
XLA Ops:
  0.0 0.0 copy-start.5
  0.0 0.0 copy-start.3
  0.0 0.0 copy-start.1
  0.0 0.0 copy-start.2
  0.0 0.0 copy-start
  0.0 1.8 %broadcast_in_dim.2 = f32[8,16,1024]{2,1,0:T(8,128)} broadcast(f32[16,1024]{1,0:T(8,128)} %param.9), dimensions={1,2} | broadcast | bytes 589824 | tf_op jit(solution)/shard_map/broadcast_in_dim | solution.py:289
  1.8 5.2 %all-to-all-start = ((f32[8,16,1024]{2,1,0:T(8,128)}), f32[8,16,1024]{2,1,0:T(8,128)S(1)}, u32[]{:S(2)}, u32[]{:S(2)}) async-start(f32[8,16,1024]{2,1,0:T(8,128)} %broadcast_in_dim.2), calls=%async_computation | async-start | bytes 1048576 | tf_op jit(solution)/shard_map/all_to_all | solution.py:289
  7.0 0.0 copy-done.5
  7.0 0.0 copy-done.3
  7.0 0.1 copy.16
  7.2 0.0 copy-done.1
  7.2 0.0 copy-done.2
  7.2 1.7 %prepare.1 = (bf16[2,224,1360]{2,1,0:T(8,128)(2,1)S(1)}, f32[8,128]{1,0:T(8,128)S(1)}, bf16[320,176]{1,0:T(8,128)(2,1)S(1)}) custom-call(f32[9]{0:T(128)S(1)} %bitcast.30, f32[128,1024]{1,0:T(8,128)S(1)} %bitcast.28, f32[8,128]{1,0:T(8,128)S(1)} %pad.16.coeffs, f32[24,128]{1,0:T(8,128)S(1)} %pad.18.col_taps, f32[128,128]{1,0:T(8,128)S(1)} %pad.19.row_taps), custom_call_target="tpu_custom_call" | custom-call | tf_op jit(solution)/shard_map/prepare/pallas_call | solution.py:294
  8.9 0.0 copy-done
  9.0 7.1 %all-to-all-done.bands = f32[8,16,1024]{2,1,0:T(8,128)S(1)} async-done(((f32[8,16,1024]{2,1,0:T(8,128)}), f32[8,16,1024]{2,1,0:T(8,128)S(1)}, u32[]{:S(2)}, u32[]{:S(2)}) %all-to-all-start) | async-done | bytes 524320 | tf_op jit(solution)/shard_map/all_to_all | solution.py:289
  16.1 0.1 fusion.2
  16.2 2.7 %collective-permute-start.1 = (f32[80,1024]{1,0:T(8,128)S(1)}, f32[80,1024]{1,0:T(8,128)S(1)}, u32[]{:S(2)}, u32[]{:S(2)}) collective-permute-start(f32[80,1024]{1,0:T(8,128)S(1)} %get-tuple-element.23), channel_id=1, source_target_pairs={{8,0},{16,8},{24,16},{32,24},{40,32},{48,40},{56,48},{64,56},{72,6... | collective-permute-start | bytes 983048 | tf_op jit(solution)/shard_map/ppermute | solution.py:315
  18.9 7.1 %collective-permute-start = (f32[80,1024]{1,0:T(8,128)S(1)}, f32[80,1024]{1,0:T(8,128)S(1)}, u32[]{:S(2)}, u32[]{:S(2)}) collective-permute-start(f32[80,1024]{1,0:T(8,128)S(1)} %get-tuple-element.24), channel_id=1, source_target_pairs={{0,8},{8,16},{16,24},{24,32},{32,40},{40,48},{48,56},{56,64},{64,7... | collective-permute-start | bytes 983048 | tf_op jit(solution)/shard_map/ppermute | solution.py:314
  26.0 3.0 %inner.1 = f32[112,1024]{1,0:T(8,128)S(1)} custom-call(f32[8,16,1024]{2,1,0:T(8,128)S(1)} %all-to-all-done.bands, bf16[2,224,1360]{2,1,0:T(8,128)(2,1)S(1)} %get-tuple-element.12.lhs, f32[128,1024]{1,0:T(8,128)S(1)} %bitcast.26), custom_call_target="tpu_custom_call" | custom-call | tf_op jit(solution)/shard_map/inner/pallas_call | solution.py:316
  28.9 3.1 %collective-permute-done.1.below = f32[80,1024]{1,0:T(8,128)S(1)} collective-permute-done((f32[80,1024]{1,0:T(8,128)S(1)}, f32[80,1024]{1,0:T(8,128)S(1)}, u32[]{:S(2)}, u32[]{:S(2)}) %collective-permute-start.1) | collective-permute-done | bytes 327712 | tf_op jit(solution)/shard_map/ppermute | solution.py:315
  32.1 0.0 collective-permute-done.above
  32.1 7.0 %outer.1 = bf16[8,56,1024]{2,1,0:T(8,128)(2,1)} custom-call(f32[9]{0:T(128)S(1)} %bitcast.31, f32[128,1024]{1,0:T(8,128)S(1)} %bitcast.27, f32[128,1024]{1,0:T(8,128)S(1)} %bitcast.29, f32[80,1024]{1,0:T(8,128)S(1)} %collective-permute-done.above, f32[80,1024]{1,0:T(8,128)S(1)} %collective-permute-done.1.below, f32[8,16,1024]{2,1,0:T(8,128)S(1)} %all-to-all-done.bands, ...), custom_call_target="tpu_custom_call" | custom-call | tf_op jit(solution)/shard_map/outer/pallas_call | solution.py:325
  39.0 0.0 copy-start.4
  39.0 3.9 %all-to-all-start.1 = ((bf16[8,56,1024]{2,1,0:T(8,128)(2,1)}), bf16[8,56,1024]{2,1,0:T(8,128)(2,1)S(1)}, u32[]{:S(2)}, u32[]{:S(2)}) async-start(bf16[8,56,1024]{2,1,0:T(8,128)(2,1)} %outer.1), calls=%async_computation.1 | async-start | bytes 1835008 | tf_op jit(solution)/shard_map/all_to_all | solution.py:343
  43.6 0.0 copy-done.4
  43.6 0.1 copy.11
  43.7 0.1 reshape.14.shifts
  43.9 12.4 %all-to-all-done.1.windows = bf16[8,56,1024]{2,1,0:T(8,128)(2,1)S(1)} async-done(((bf16[8,56,1024]{2,1,0:T(8,128)(2,1)}), bf16[8,56,1024]{2,1,0:T(8,128)(2,1)S(1)}, u32[]{:S(2)}, u32[]{:S(2)}) %all-to-all-start.1) | async-done | bytes 917536 | tf_op jit(solution)/shard_map/all_to_all | solution.py:343
  56.3 5.8 %search.1 = f32[16,1024]{1,0:T(8,128)} custom-call(s32[1]{0:T(128)S(6)} %copy.21.count, s32[384]{0:T(512)S(1)} %reshape.14.shifts, bf16[8,56,1024]{2,1,0:T(8,128)(2,1)S(1)} %all-to-all-done.1.windows), custom_call_target="tpu_custom_call" | custom-call | tf_op jit(solution)/shard_map/search/pallas_call | solution.py:344
  (9 shorter events, 0.1 us)
Async XLA Ops:
  0.0 7.0 %copy-start.5 = (f32[1,1,27,3]{2,1,3,0:T(1,128)S(1)}, f32[1,1,27,3]{2,1,3,0:T(1,128)}, u32[]{:S(2)}) copy-start(f32[1,1,27,3]{2,1,3,0:T(1,128)} %param.11) | copy-start | bytes 976
  0.0 7.0 %copy-start.3 = (f32[2,27,17]{1,0,2:T(2,128)S(1)}, f32[2,27,17]{1,0,2:T(2,128)}, u32[]{:S(2)}) copy-start(f32[2,27,17]{1,0,2:T(2,128)} %param.10) | copy-start | bytes 11020
  0.0 7.2 %copy-start.1 = (f32[1,128,1024]{2,1,0:T(8,128)S(1)}, f32[1,128,1024]{2,1,0:T(8,128)}, u32[]{:S(2)}) copy-start(f32[1,128,1024]{2,1,0:T(8,128)} %param.13) | copy-start | bytes 1572868
  0.0 7.2 %copy-start.2 = (f32[1,9]{1,0:T(1,128)S(1)}, f32[1,9]{1,0:T(1,128)}, u32[]{:S(2)}) copy-start(f32[1,9]{1,0:T(1,128)} %param.12) | copy-start | bytes 112
  0.0 8.9 %copy-start = (f32[1,128,1024]{2,1,0:T(8,128)S(1)}, f32[1,128,1024]{2,1,0:T(8,128)}, u32[]{:S(2)}) copy-start(f32[1,128,1024]{2,1,0:T(8,128)} %param.8) | copy-start | bytes 1572868
  1.8 14.3 %all-to-all-start = ((f32[8,16,1024]{2,1,0:T(8,128)}), f32[8,16,1024]{2,1,0:T(8,128)S(1)}, u32[]{:S(2)}, u32[]{:S(2)}) async-start(f32[8,16,1024]{2,1,0:T(8,128)} %broadcast_in_dim.2), calls=%async_computation | async-start | bytes 1048576 | tf_op jit(solution)/shard_map/all_to_all | solution.py:289
  16.2 15.9 %collective-permute-start.1 = (f32[80,1024]{1,0:T(8,128)S(1)}, f32[80,1024]{1,0:T(8,128)S(1)}, u32[]{:S(2)}, u32[]{:S(2)}) collective-permute-start(f32[80,1024]{1,0:T(8,128)S(1)} %get-tuple-element.23), channel_id=1, source_target_pairs={{8,0},{16,8},{24,16},{32,24},{40,32},{48,40},{56,48},{64,56},{72,6... | collective-permute-start | bytes 983048 | tf_op jit(solution)/shard_map/ppermute | solution.py:315
  18.9 13.2 %collective-permute-start = (f32[80,1024]{1,0:T(8,128)S(1)}, f32[80,1024]{1,0:T(8,128)S(1)}, u32[]{:S(2)}, u32[]{:S(2)}) collective-permute-start(f32[80,1024]{1,0:T(8,128)S(1)} %get-tuple-element.24), channel_id=1, source_target_pairs={{0,8},{8,16},{16,24},{24,32},{32,40},{40,48},{48,56},{56,64},{64,7... | collective-permute-start | bytes 983048 | tf_op jit(solution)/shard_map/ppermute | solution.py:314
  39.0 4.6 %copy-start.4 = (s32[1,24,8,2]{1,3,2,0:T(2,128)S(1)}, s32[1,24,8,2]{1,3,2,0:T(2,128)}, u32[]{:S(2)}) copy-start(s32[1,24,8,2]{1,3,2,0:T(2,128)} %param.14) | copy-start | bytes 4612
  39.0 17.2 %all-to-all-start.1 = ((bf16[8,56,1024]{2,1,0:T(8,128)(2,1)}), bf16[8,56,1024]{2,1,0:T(8,128)(2,1)S(1)}, u32[]{:S(2)}, u32[]{:S(2)}) async-start(bf16[8,56,1024]{2,1,0:T(8,128)(2,1)} %outer.1), calls=%async_computation.1 | async-start | bytes 1835008 | tf_op jit(solution)/shard_map/all_to_all | solution.py:343

commit v2 on v1

v2 whole, which is shorter than its diff:
```python
import jax
import jax.numpy as jnp
from jax import lax
from jax.experimental import pallas as pl
from jax.experimental.pallas import tpu as pltpu
from jax.sharding import PartitionSpec as P

NB = 27
R = 8
F = 4
SMAX = 16
EPOCHS = 8
H = 128
W = 1024
BAND = 16
TAPS = 2 * R + 1
PTAPS = 2 * F + 1
VEDGE = 24
TEDGE = 32
MID = 56
MWIN = 80
EDGE = 32
EWIN = 48
NBLK = 256
PADW = W + 128
OUTR = 56
IROWS = H - 2 * BAND
OROWS = 2 * BAND
CWIN = 2 * NBLK
MIDDLE = (H - 1) / 2.0
f32 = jnp.float32
bf16 = jnp.bfloat16


def toeplitz(coeff_rows, col_taps, row_taps, table):
    scaled = [col_taps * rows[p:p + 1, :] for rows in coeff_rows for p in range(3)]
    profiles = jnp.dot(jnp.concatenate(scaled, axis=0), row_taps,
                       precision=lax.Precision.HIGHEST, preferred_element_type=f32)
    for s in range(8):
        moved = profiles if s == 0 else pltpu.roll(profiles, s, 1)
        for i in range(len(scaled)):
            table[i, pl.ds(s, 24, stride=8), :] = moved[24 * i:24 * i + 24]


def band_rows(table, at, window, offset, first_row, lanes, store):
    lane = lax.broadcasted_iota(jnp.int32, (8, 128), 1)
    row = lax.broadcasted_iota(jnp.int32, (8, 128), 0) + first_row
    w = (row.astype(f32) - MIDDLE) / MIDDLE
    for q in range((lanes + 127) // 128):
        even, odd = jnp.zeros((8, 128), f32), jnp.zeros((8, 128), f32)
        for l in range(TAPS):
            a = l * window + offset
            low = a % 128
            if a // 128 == q:
                keep = None if low + 24 <= 128 else lane >= low
            elif (a + 23) // 128 == q:
                keep = lane < 24
            else:
                continue
            parts = []
            for p in range(3):
                piece = table[at + p, 8 * l:8 * l + 8, :]
                if low:
                    piece = pltpu.roll(piece, low, 1)
                if keep is not None:
                    piece = jnp.where(keep, piece, 0.0)
                parts.append(piece)
            even = even + (parts[0] + w * parts[2])
            odd = odd + parts[1]
        store(q, even, odd)


def split(x):
    hi = x.astype(bf16)
    return hi, (x - hi.astype(f32)).astype(bf16)


def shift_band(band, hi_ref, lo_ref, at, copies=None, copy_at=0):
    blank = jnp.zeros((BAND, PADW - W), bf16)
    for i, (piece, ref) in enumerate(zip(split(band), (hi_ref, lo_ref))):
        piece = jnp.concatenate([piece, blank], axis=1)
        for l in range(TAPS):
            moved = piece if l == R else pltpu.roll(piece, (R - l) % PADW, 1)
            ref[l, at:at + BAND, :] = moved[:, 0:W]
            if copies:
                copies[i][l, copy_at:copy_at + BAND, :] = moved[:, 0:W]


def model_block(lhs, hi_ref, lo_ref, rows, count, n):
    cols = slice(n * NBLK, (n + 1) * NBLK)
    depth = TAPS * (rows.stop - rows.start)
    acc = jnp.dot(lhs, hi_ref[:, rows, cols].reshape(depth, NBLK), preferred_element_type=f32)
    acc = acc[0:2 * count] + acc[2 * count:4 * count] + jnp.dot(
        lhs[0:2 * count], lo_ref[:, rows, cols].reshape(depth, NBLK), preferred_element_type=f32)
    col = lax.broadcasted_iota(jnp.int32, (count, NBLK), 1) + n * NBLK
    u = (col.astype(f32) - (W - 1) / 2.0) / ((W - 1) / 2.0)
    return acc[0:count] + u * acc[count:2 * count]


def filter_matrices(psf, inner_rows, outer_rows, cols, wide):
    lane = lax.broadcasted_iota(jnp.int32, (8, 128), 1)
    sub = lax.broadcasted_iota(jnp.int32, (8, 128), 0)
    taps = jnp.zeros((8, 128), f32)
    for k in range(PTAPS):
        taps = jnp.where(lane - sub == k, psf[k], taps)
    for g in range(IROWS // 8):
        wide[8 * g:8 * g + 8, :] = pltpu.roll(taps, 8 * g + 4, 1)[:, 0:2 * MID]
    for rows, depth, ref in ((IROWS, 2 * MID, inner_rows), (OROWS, EWIN, outer_rows)):
        hi, lo = split(wide[0:rows, 0:depth])
        ref[0:rows, :] = hi
        ref[rows:2 * rows, :] = lo
    for at in range(0, CWIN, 128):
        offset = lax.broadcasted_iota(jnp.int32, (128, NBLK), 0) - lax.broadcasted_iota(jnp.int32, (128, NBLK), 1) + (at - 124)
        block = jnp.zeros((128, NBLK), f32)
        for k in range(PTAPS):
            block = jnp.where(offset == k, psf[k], block)
        hi, lo = split(block)
        cols[0, at:at + 128, :] = hi
        cols[1, at:at + 128, :] = lo


def filter_cols(count, halves, col_filter, store):
    for n in range(W // NBLK):
        window = slice(n * NBLK, n * NBLK + CWIN)
        acc = jnp.dot(halves[:, window], col_filter[0], preferred_element_type=f32)
        acc = acc[0:count] + acc[count:2 * count] + jnp.dot(
            halves[0:count, window], col_filter[1], preferred_element_type=f32)
        store(slice(n * NBLK, (n + 1) * NBLK), acc)


def filter_rows(count, matrix, rows):
    hi, lo = split(rows)
    acc = jnp.dot(matrix[...], hi, preferred_element_type=f32)
    return acc[0:count] + acc[count:2 * count] + jnp.dot(matrix[0:count, :], lo, preferred_element_type=f32)


def clear_margins(halves):
    blank = jnp.zeros((halves.shape[0], 128), bf16)
    halves[:, 0:128] = blank
    halves[:, W + 128:W + 256] = blank


def prepare_kernel(psf, inv_var, coeffs, col_taps, row_taps, lhs, weight, inner_rows, outer_rows, cols,
                   table, wide, psf_wide):
    filter_matrices(psf, inner_rows, outer_rows, cols, psf_wide)
    toeplitz([coeffs[...]], col_taps[...], row_taps[...], table)
    lanes = TAPS * MWIN
    for block in range(2):
        for g in range(MID // 8):
            def store(q, even, odd, block=block, g=g):
                end = min(128, lanes - q * 128)
                wide[block, 8 * g:8 * g + 8, q * 128:q * 128 + end] = even[:, 0:end]
                wide[block, MID + 8 * g:MID + 8 * g + 8, q * 128:q * 128 + end] = odd[:, 0:end]
            band_rows(table, 0, MWIN, 8 * g + 8 * block, 8 + MID * block + 8 * g, lanes, store)
        hi, lo = split(wide[block])
        lhs[block, 0:2 * MID, :] = hi
        lhs[block, 2 * MID:4 * MID, :] = lo
    power = psf[0] * psf[0]
    for k in range(1, PTAPS):
        power = power + psf[k] * psf[k]
    weight[...] = jnp.full((8, 128), power * power * (jnp.sum(inv_var[...]) / (H * W)), f32)


def inner_kernel(bands, lhs, visits, inv_var, row_filter, col_filter,
                 filtered, diff_edges, hi_edges, lo_edges, hi_ref, lo_ref, diff, halves):
    for e in range(EPOCHS):
        copies = None if 0 < e < EPOCHS - 1 else (hi_edges, lo_edges)
        shift_band(bands[e], hi_ref, lo_ref, e * BAND, copies, 0 if e == 0 else BAND)
    clear_margins(halves)
    for n in range(W // NBLK):
        cols = slice(n * NBLK, (n + 1) * NBLK)
        for block in range(2):
            rows = slice(0, MWIN) if block == 0 else slice(H - MWIN, H)
            model = model_block(lhs[block], hi_ref, lo_ref, rows, MID, n)
            diff[MID * block:MID * (block + 1), cols] = visits[8 + MID * block:8 + MID * (block + 1), cols] - model
        hi, lo = split(filter_rows(IROWS, row_filter, diff[:, cols]))
        halves[0:IROWS, 128 + n * NBLK:128 + (n + 1) * NBLK] = hi
        halves[IROWS:2 * IROWS, 128 + n * NBLK:128 + (n + 1) * NBLK] = lo
    diff_edges[0:BAND, :] = diff[0:BAND, :]
    diff_edges[BAND:2 * BAND, :] = diff[2 * MID - BAND:2 * MID, :]

    def store(cols, values):
        filtered[:, cols] = (values * inv_var[BAND:H - BAND, cols]).astype(bf16)
    filter_cols(IROWS, halves, col_filter, store)


def outer_kernel(visits, inv_var, above, below, t_above, t_below, filtered, diff_edges, hi_edges, lo_edges, coeffs,
                 col_taps, row_taps, weight, row_filter, col_filter,
                 out, table, wide, lhs, hi_ref, lo_ref, diff, halves, ends, last, sems):
    first = weight[...].astype(bf16)
    rest = weight[...] - first.astype(f32)
    second = rest.astype(bf16)
    third = (rest - second.astype(f32)).astype(bf16)
    last[...] = jnp.concatenate([first, second, third, jnp.zeros((8, W - 384), bf16)], axis=1)
    early, late = [], []
    for owner in range(EPOCHS):
        for part in range(3):
            chunk = owner + part
            inside = 2 <= chunk < 8
            source = filtered.at[16 * (chunk - 2):16 * (chunk - 1), :] if inside else ends.at[(0, 1, 8, 9).index(chunk)]
            copy = pltpu.make_async_copy(source, out.at[owner, part * 16:(part + 1) * 16, :], sems.at[owner * 4 + part])
            (early if inside else late).append(copy)
        early.append(pltpu.make_async_copy(last, out.at[owner, 48:OUTR, :], sems.at[owner * 4 + 3]))
    for copy in early:
        copy.start()
    toeplitz([above[40:48, 0:128], coeffs[...], below[40:48, 0:128]], col_taps[...], row_taps[...], table)
    lanes = TAPS * EWIN
    for block in range(2):
        for g in range(4):
            if block == 0:
                at, first = (0, H - VEDGE + 8 * g) if g < 3 else (3, 0)
            else:
                at, first = (6, 8 * (g - 1)) if g > 0 else (3, H - 8)

            def store(q, even, odd, block=block, g=g):
                end = min(128, lanes - q * 128)
                wide[block, 8 * g:8 * g + 8, q * 128:q * 128 + end] = even[:, 0:end]
                wide[block, EDGE + 8 * g:EDGE + 8 * g + 8, q * 128:q * 128 + end] = odd[:, 0:end]
            band_rows(table, at, EWIN, 8 * g, first, lanes, store)
        hi, lo = split(wide[block])
        lhs[block, 0:2 * EDGE, :] = hi
        lhs[block, 2 * EDGE:4 * EDGE, :] = lo
    for edges, ref in ((hi_edges, hi_ref), (lo_edges, lo_ref)):
        for l in range(TAPS):
            ref[l, 32:64, :] = edges[l]
    shift_band(t_above[0:16, :], hi_ref, lo_ref, 0)
    shift_band(t_above[16:32, :], hi_ref, lo_ref, 16)
    shift_band(t_below[0:16, :], hi_ref, lo_ref, 64)
    shift_band(t_below[16:32, :], hi_ref, lo_ref, 80)
    clear_margins(halves)
    diff[0, EDGE:EWIN, :] = diff_edges[0:BAND, :]
    diff[1, 0:BAND, :] = diff_edges[BAND:2 * BAND, :]
    for n in range(W // NBLK):
        cols = slice(n * NBLK, (n + 1) * NBLK)
        model = model_block(lhs[0], hi_ref, lo_ref, slice(0, EWIN), EDGE, n)
        diff[0, 0:VEDGE, cols] = above[0:VEDGE, cols] - model[0:VEDGE]
        diff[0, VEDGE:EDGE, cols] = visits[0:8, cols] - model[VEDGE:EDGE]
        model = model_block(lhs[1], hi_ref, lo_ref, slice(EWIN, 2 * EWIN), EDGE, n)
        diff[1, BAND:BAND + 8, cols] = visits[H - 8:H, cols] - model[0:8]
        diff[1, BAND + 8:EWIN, cols] = below[0:VEDGE, cols] - model[8:EDGE]
        for end in range(2):
            hi, lo = split(filter_rows(OROWS, row_filter, diff[end, :, cols]))
            halves[OROWS * end:OROWS * end + OROWS, 128 + n * NBLK:128 + (n + 1) * NBLK] = hi
            halves[OROWS * (2 + end):OROWS * (3 + end), 128 + n * NBLK:128 + (n + 1) * NBLK] = lo

    def store(cols, values):
        scales = (above[24:40, cols], inv_var[0:BAND, cols], inv_var[H - BAND:H, cols], below[24:40, cols])
        for i in range(4):
            ends[i, :, cols] = (values[16 * i:16 * i + 16] * scales[i]).astype(bf16)
    filter_cols(2 * OROWS, halves, col_filter, store)
    for copy in late:
        copy.start()
    for copy in early + late:
        copy.wait()


def search_kernel(count, starts, across_of, windows, out, table, packed):
    weight_sum = jnp.zeros((8, 128), f32)
    for e in range(EPOCHS):
        rows = windows[e, 0:48, :].astype(f32)
        for q in range(8):
            table[e, pl.ds(q, 48, stride=8), :] = rows[:, q * 128:(q + 1) * 128]
        packed[768 * e:768 * e + 384, :] = table[e].astype(bf16)
        packed[768 * e + 384:768 * e + 752, :] = table[e, 8:376, :].astype(bf16)
        for q in range(3):
            weight_sum = weight_sum + windows[e, 48:OUTR, q * 128:(q + 1) * 128].astype(f32)
    lane = lax.broadcasted_iota(jnp.int32, (8, 128), 1)
    sub = lax.broadcasted_iota(jnp.int32, (8, 128), 0)
    right = (lane >= 64)[None]
    from_next = ((lane >= 64) & (sub < 7))[None]
    from_last = ((lane < 64) & (sub > 0))[None]

    def stack(v, half):
        whole = jnp.zeros((8, 8, 128), f32)
        inside = jnp.zeros((8, 8, 128), f32)
        for e in range(EPOCHS):
            across = across_of[v * EPOCHS + e]
            first = pl.multiple_of(starts[v * EPOCHS + e] + 64 * half, 16)
            window = packed[pl.ds(first, 64), :]
            moved = pltpu.roll(window, (-across) & 127, 1).astype(f32).reshape(8, 8, 128)
            source = lane + across
            keep = ((source >= 0) & (source < 128))[None]
            whole = whole + moved
            inside = inside + jnp.where(keep, moved, 0.0)
        outside = whole - inside
        total = inside + jnp.where(from_next, pltpu.roll(outside, 7, 1), 0.0)
        return total + jnp.where(from_last, pltpu.roll(outside, 1, 1), 0.0)

    most = count[0] - 1

    def step(turn, best):
        first, second = 2 * turn, jnp.minimum(2 * turn + 1, most)
        tops = jnp.maximum(best[0], jnp.maximum(stack(first, 0), stack(second, 0)))
        lows = jnp.maximum(best[1], jnp.maximum(stack(first, 1), stack(second, 1)))
        return tops, lows

    least = jnp.full((8, 8, 128), -1e30, f32)
    best = lax.fori_loop(0, (count[0] + 1) // 2, step, (least, least))
    norm = jnp.sqrt(weight_sum)[None]
    for half in range(2):
        table[0, half * 64:half * 64 + 64, :] = (best[half] / norm).reshape(64, 128)
    for q in range(8):
        out[:, q * 128:(q + 1) * 128] = table[0, pl.ds(q, BAND, stride=8), :]


def vmem(count):
    return [pl.BlockSpec(memory_space=pltpu.VMEM)] * count


def smem(count):
    return [pl.BlockSpec(memory_space=pltpu.SMEM)] * count


def shape(*dims, dtype=f32):
    return jax.ShapeDtypeStruct(dims, dtype)


def held(x):
    return pltpu.with_memory_space_constraint(x, pltpu.VMEM)


def to_neighbours(downward, upward):
    tiles = lax.axis_size("sky")
    above = lax.ppermute(downward, "sky", [(i, i + 1) for i in range(tiles - 1)])
    below = lax.ppermute(upward, "sky", [(i + 1, i) for i in range(tiles - 1)])
    return held(above), held(below)


def on_device(visits, template, basis_taps, coeffs, psf_taps, inv_var, shifts, vel_count):
    visits, inv_var, psf = visits[0], inv_var[0], psf_taps[0]
    epochs = lax.axis_size("epoch")
    bands = lax.all_to_all(jnp.broadcast_to(template[None], (epochs, BAND, W)), "epoch", 0, 0, tiled=True)
    own = jnp.pad(coeffs[0, 0].T, ((0, 5), (0, 128 - NB)))
    wide = jnp.pad(own, ((0, 0), (0, W - 128)))
    above, below = to_neighbours(
        jnp.concatenate([visits[H - VEDGE:], inv_var[H - SMAX:], wide], axis=0),
        jnp.concatenate([visits[:VEDGE], inv_var[:SMAX], wide], axis=0),
    )
    col_taps = jnp.pad(basis_taps[1].T, ((0, 24 - TAPS), (0, 128 - NB)))
    row_taps = jnp.pad(basis_taps[0], ((0, 128 - NB), (0, 128 - TAPS)))
    lhs, weight, inner_rows, outer_rows, col_filter = pl.pallas_call(
        prepare_kernel,
        out_shape=(
            pltpu.VMEM((2, 4 * MID, TAPS * MWIN), bf16),
            shape(8, 128),
            pltpu.VMEM((2 * IROWS, 2 * MID), bf16),
            pltpu.VMEM((2 * OROWS, EWIN), bf16),
            pltpu.VMEM((2, CWIN, NBLK), bf16),
        ),
        in_specs=smem(1) + vmem(4),
        out_specs=tuple(vmem(5)),
        scratch_shapes=[
            pltpu.VMEM((3, 192, 128), f32),
            pltpu.VMEM((2, 2 * MID, TAPS * MWIN), f32),
            pltpu.VMEM((IROWS, 2 * MID), f32),
        ],
        compiler_params=pltpu.CompilerParams(vmem_limit_bytes=8 << 20),
        name="prepare",
    )(psf, held(inv_var), held(own), held(col_taps), held(row_taps))
    bands, weight = lax.optimization_barrier((bands, weight))
    t_above, t_below = to_neighbours(bands[6:].reshape(TEDGE, W), bands[:2].reshape(TEDGE, W))
    filtered, diff_edges, hi_edges, lo_edges = pl.pallas_call(
        inner_kernel,
        out_shape=(
            pltpu.VMEM((IROWS, W), bf16),
            pltpu.VMEM((2 * BAND, W), f32),
            pltpu.VMEM((TAPS, 2 * BAND, W), bf16),
            pltpu.VMEM((TAPS, 2 * BAND, W), bf16),
        ),
        in_specs=vmem(6),
        out_specs=tuple(vmem(4)),
        scratch_shapes=[
            pltpu.VMEM((TAPS, H, W), bf16),
            pltpu.VMEM((TAPS, H, W), bf16),
            pltpu.VMEM((2 * MID, W), f32),
            pltpu.VMEM((2 * IROWS, W + 256), bf16),
        ],
        compiler_params=pltpu.CompilerParams(vmem_limit_bytes=24 << 20),
        name="inner",
    )(held(bands), lhs, held(visits), held(inv_var), inner_rows, col_filter)
    windows = pl.pallas_call(
        outer_kernel,
        out_shape=shape(EPOCHS, OUTR, W, dtype=bf16),
        in_specs=vmem(16),
        out_specs=pl.BlockSpec(memory_space=pl.ANY),
        scratch_shapes=[
            pltpu.VMEM((9, 192, 128), f32),
            pltpu.VMEM((2, 2 * EDGE, TAPS * EWIN), f32),
            pltpu.VMEM((2, 4 * EDGE, TAPS * EWIN), bf16),
            pltpu.VMEM((TAPS, 2 * EWIN, W), bf16),
            pltpu.VMEM((TAPS, 2 * EWIN, W), bf16),
            pltpu.VMEM((2, EWIN, W), f32),
            pltpu.VMEM((4 * OROWS, W + 256), bf16),
            pltpu.VMEM((4, BAND, W), bf16),
            pltpu.VMEM((8, W), bf16),
            pltpu.SemaphoreType.DMA((4 * EPOCHS,)),
        ],
        compiler_params=pltpu.CompilerParams(vmem_limit_bytes=24 << 20),
        name="outer",
    )(held(visits), held(inv_var), above, below, t_above, t_below, filtered, diff_edges, hi_edges, lo_edges,
      held(own), held(col_taps), held(row_taps), held(weight), outer_rows, col_filter)
    down = shifts[0, :, :, 0] + SMAX
    starts = jnp.arange(EPOCHS, dtype=jnp.int32) * 768 + (down & 1) * 384 + (down - (down & 1)) * 8
    moved = lax.all_to_all(windows, "epoch", 0, 0, tiled=True)
    return pl.pallas_call(
        search_kernel,
        out_shape=shape(BAND, W),
        in_specs=smem(3) + vmem(1),
        out_specs=vmem(1)[0],
        scratch_shapes=[pltpu.VMEM((EPOCHS, 384, 128), f32), pltpu.VMEM((2 * EPOCHS * 384, 128), bf16)],
        compiler_params=pltpu.CompilerParams(vmem_limit_bytes=12 << 20),
        name="search",
    )(vel_count, starts.reshape(-1), shifts[0, :, :, 1].reshape(-1), held(moved))


def solution(mesh):
    in_specs = (
        P("epoch", "sky", None),
        P(("sky", "epoch"), None),
        P(),
        P("epoch", "sky", None, None),
        P("epoch", None),
        P("epoch", "sky", None),
        P("sky", None, None, None),
        P("sky"),
    )
    out_specs = P(("sky", "epoch"), None)
    return jax.shard_map(
        on_device, mesh=mesh, in_specs=in_specs, out_specs=out_specs, check_vma=False
    )
```

time: 62.1 us -> 59.2 us (0.953)
  the two profiles are of different devices: /device:TPU:249 before, /device:TPU:256 now
where the time goes in v2:
time: 59.2 us; the launch traced here: 58.8 us
  starting transfers between devices  30.7 us (52%)
  Pallas kernels  15.1 us (26%)
  waiting for transfers between devices  8.88 us (15%)
  local copies, waits for them, and re-layouts  2.41 us (4%)
  between operations  0.9 us (2%)
  other arithmetic  0.8 us (1%)
    ppermute x2, starting transfers between devices, to_neighbours(): below = lax.ppermute(upward, 'sky', [(i + 1, i) for i in range(tiles - 1)])  15.7 us
    all_to_all x1, waiting for transfers between devices, on_device(): moved = lax.all_to_all(windows, 'epoch', 0, 0, tiled=True)  8.87 us
    all_to_all x1, starting transfers between devices, on_device(): moved = lax.all_to_all(windows, 'epoch', 0, 0, tiled=True)  5.7 us
    pallas_call x1, Pallas kernels, on_device(): pl.pallas_call(outer_kernel, out_shape=shape(EPOCHS, OUTR, W, dtype=bf16)...  5.56 us
    all_to_all x1, starting transfers between devices, on_device(): lax.all_to_all(jnp.broadcast_to(template[None], (epochs, BAND, W)), 'epoc...  5.44 us
    pallas_call x1, Pallas kernels, on_device(): pl.pallas_call(search_kernel, out_shape=shape(BAND, W), in_specs=smem(3)...  3.97 us
    ppermute x2, starting transfers between devices, to_neighbours(): lax.ppermute(downward, 'sky', [(i, i + 1) for i in range(tiles - 1)])  3.83 us
    pallas_call x1, Pallas kernels, on_device(): pl.pallas_call(inner_kernel, out_shape=(pltpu.VMEM((IROWS, W), bf16), plt...  3.81 us
  transfers between devices with their start and end apart: 6, of which 1 were waited for; matrix products, arithmetic and copies ran while one was open for 2% of the time, Pallas kernels for 9%

profile of v2, /device:TPU:256, one launch (start us, length us, event | category | flops | bytes accessed | tf_op | source)
XLA Modules:
  0.0 58.8 jit_solution(14014248357423888023)
XLA Ops:
  0.0 0.0 copy-start.5
  0.0 0.0 copy-start
  0.0 0.0 copy-start.1
  0.0 1.8 %broadcast_in_dim.2 = f32[8,16,1024]{2,1,0:T(8,128)} broadcast(f32[16,1024]{1,0:T(8,128)} %param.9), dimensions={1,2} | broadcast | bytes 589824 | tf_op jit(solution)/shard_map/broadcast_in_dim | solution.py:332
  1.8 0.0 copy-start.3
  1.8 0.0 copy-start.2
  1.8 5.4 %all-to-all-start = ((f32[8,16,1024]{2,1,0:T(8,128)}), f32[8,16,1024]{2,1,0:T(8,128)S(1)}, u32[]{:S(2)}, u32[]{:S(2)}) async-start(f32[8,16,1024]{2,1,0:T(8,128)} %broadcast_in_dim.2), calls=%async_computation | async-start | bytes 1048576 | tf_op jit(solution)/shard_map/all_to_all | solution.py:332
  7.2 0.0 copy-done.5
  7.3 0.0 copy-done
  7.3 0.0 copy-done.1
  7.3 0.8 %fusion.1 = (f32[48,1024]{1,0:T(8,128)}, f32[48,1024]{1,0:T(8,128)}) fusion(f32[8,128]{1,0:T(8,128)S(1)} %pad.16.coeffs, f32[16,1024]{1,0:T(8,128)S(1)} %get-tuple-element.31, f32[24,1024]{1,0:T(8,128)S(1)} %get-tuple-element.29, f32[16,1024]{1,0:T(8,128)S(1)} %get-tuple-element.32, f32[24,1024]{1,0:T(8,128)S(1)} %get-tuple-element.30), kind=kLoop, calls=%fused_computation.3 | loop fusion | flops 294912 | bytes 724992 | tf_op jit(solution)/shard_map/concatenate | solution.py:337
  8.1 1.9 %collective-permute-start = (f32[48,1024]{1,0:T(8,128)}, f32[48,1024]{1,0:T(8,128)}, u32[]{:S(2)}, u32[]{:S(2)}) collective-permute-start(f32[48,1024]{1,0:T(8,128)} %get-tuple-element.38), channel_id=1, source_target_pairs={{0,8},{8,16},{16,24},{24,32},{32,40},{40,48},{48,56},{56,64},{64,7... | collective-permute-start | bytes 589832 | tf_op jit(solution)/shard_map/ppermute | solution.py:324
  10.0 7.9 %collective-permute-start.1 = (f32[48,1024]{1,0:T(8,128)}, f32[48,1024]{1,0:T(8,128)}, u32[]{:S(2)}, u32[]{:S(2)}) collective-permute-start(f32[48,1024]{1,0:T(8,128)} %get-tuple-element.37), channel_id=1, source_target_pairs={{8,0},{16,8},{24,16},{32,24},{40,32},{48,40},{56,48},{64,56},{72,6... | collective-permute-start | bytes 589832 | tf_op jit(solution)/shard_map/ppermute | solution.py:325
  17.9 0.0 copy-done.3
  17.9 0.1 copy.23
  18.1 0.0 copy-done.2
  18.1 1.7 %prepare.1 = (bf16[2,224,1360]{2,1,0:T(8,128)(2,1)S(1)}, f32[8,128]{1,0:T(8,128)S(1)}, bf16[192,112]{1,0:T(8,128)(2,1)S(1)}, bf16[64,48]{1,0:T(8,128)(2,1)S(1)}, bf16[2,512,256]{2,1,0:T(8,128)(2,1)S(1)}) custom-call(f32[9]{0:T(128)S(1)} %bitcast.38, f32[128,1024]{1,0:T(8,128)S(1)} %bitcast.33, f32[8,128]{1,0:T(8,128)S(1)} %pad.16.coeffs, ...), custom_call_target="tpu_custom_call" | custom-call | tf_op jit(solution)/shard_map/prepare/pallas_call | solution.py:341
  19.8 0.0 all-to-all-done.bands
  19.9 1.9 %collective-permute-start.2 = (f32[32,1024]{1,0:T(8,128)S(1)}, f32[32,1024]{1,0:T(8,128)S(1)}, u32[]{:S(2)}, u32[]{:S(2)}) collective-permute-start(f32[32,1024]{1,0:T(8,128)S(1)} %bitcast.40), channel_id=1, source_target_pairs={{0,8},{8,16},{16,24},{24,32},{32,40},{40,48},{48,56},{56,64},{64,7... | collective-permute-start | bytes 393224 | tf_op jit(solution)/shard_map/ppermute | solution.py:324
  21.8 7.9 %collective-permute-start.3 = (f32[32,1024]{1,0:T(8,128)S(1)}, f32[32,1024]{1,0:T(8,128)S(1)}, u32[]{:S(2)}, u32[]{:S(2)}) collective-permute-start(f32[32,1024]{1,0:T(8,128)S(1)} %bitcast.39), channel_id=1, source_target_pairs={{8,0},{16,8},{24,16},{32,24},{40,32},{48,40},{56,48},{64,56},{72,6... | collective-permute-start | bytes 393224 | tf_op jit(solution)/shard_map/ppermute | solution.py:325
  29.7 3.8 %inner.1 = (bf16[96,1024]{1,0:T(8,128)(2,1)S(1)}, f32[32,1024]{1,0:T(8,128)S(1)}, bf16[17,32,1024]{2,1,0:T(8,128)(2,1)S(1)}, bf16[17,32,1024]{2,1,0:T(8,128)(2,1)S(1)}) custom-call(f32[8,16,1024]{2,1,0:T(8,128)S(1)} %all-to-all-done.bands, bf16[2,224,1360]{2,1,0:T(8,128)(2,1)S(1)} %get-tuple-element.18.lhs, f32[128,1024]{1,0:T(8,128)S(1)} %bitcast.36, ...), custom_call_target="tpu_custom_call" | custom-call | tf_op jit(solution)/shard_map/inner/pallas_call | solution.py:362
  33.5 0.0 collective-permute-done.above
  33.5 0.0 collective-permute-done.1.below
  33.5 0.0 collective-permute-done.2.t_above
  33.5 0.0 collective-permute-done.3.t_below
  33.5 5.6 %outer.1 = bf16[8,56,1024]{2,1,0:T(8,128)(2,1)} custom-call(f32[128,1024]{1,0:T(8,128)S(1)} %bitcast.37, f32[128,1024]{1,0:T(8,128)S(1)} %bitcast.35, f32[48,1024]{1,0:T(8,128)} %collective-permute-done.above, f32[48,1024]{1,0:T(8,128)} %collective-permute-done.1.below, f32[32,1024]{1,0:T(8,128)S(1)} %collective-permute-done.2.t_above, ...), custom_call_target="tpu_custom_call" | custom-call | tf_op jit(solution)/shard_map/outer/pallas_call | solution.py:381
  39.1 0.0 copy-start.4
  39.1 5.7 %all-to-all-start.1 = ((bf16[8,56,1024]{2,1,0:T(8,128)(2,1)}), bf16[8,56,1024]{2,1,0:T(8,128)(2,1)S(1)}, u32[]{:S(2)}, u32[]{:S(2)}) async-start(bf16[8,56,1024]{2,1,0:T(8,128)(2,1)} %outer.1), calls=%async_computation.1 | async-start | bytes 1835008 | tf_op jit(solution)/shard_map/all_to_all | solution.py:404
  44.8 0.0 copy-done.4
  44.8 0.1 copy.16
  44.9 0.1 add.37
  45.0 0.1 add.34
  45.1 0.1 copy.17
  45.2 0.1 reshape_squeeze.3.across_of
  45.9 8.9 %all-to-all-done.1.windows = bf16[8,56,1024]{2,1,0:T(8,128)(2,1)S(1)} async-done(((bf16[8,56,1024]{2,1,0:T(8,128)(2,1)}), bf16[8,56,1024]{2,1,0:T(8,128)(2,1)S(1)}, u32[]{:S(2)}, u32[]{:S(2)}) %all-to-all-start.1) | async-done | bytes 917536 | tf_op jit(solution)/shard_map/all_to_all | solution.py:404
  54.8 4.0 %search.1 = f32[16,1024]{1,0:T(8,128)} custom-call(s32[1]{0:T(128)S(6)} %copy.28.count, s32[192]{0:T(256)S(1)} %fusion.3.starts, s32[192]{0:T(256)S(1)} %reshape_squeeze.3.across_of, bf16[8,56,1024]{2,1,0:T(8,128)(2,1)S(1)} %all-to-all-done.1.windows), custom_call_target="tpu_custom_call" | custom-call | tf_op jit(solution)/shard_map/search/pallas_call | solution.py:405
  (14 shorter events, 0.1 us)
Async XLA Ops:
  0.0 7.2 %copy-start.5 = (f32[1,1,27,3]{2,1,3,0:T(1,128)S(1)}, f32[1,1,27,3]{2,1,3,0:T(1,128)}, u32[]{:S(2)}) copy-start(f32[1,1,27,3]{2,1,3,0:T(1,128)} %param.11) | copy-start | bytes 976
  0.0 7.3 %copy-start = (f32[1,128,1024]{2,1,0:T(8,128)S(1)}, f32[1,128,1024]{2,1,0:T(8,128)}, u32[]{:S(2)}) copy-start(f32[1,128,1024]{2,1,0:T(8,128)} %param.13) | copy-start | bytes 1572868
  0.0 7.3 %copy-start.1 = (f32[1,128,1024]{2,1,0:T(8,128)S(1)}, f32[1,128,1024]{2,1,0:T(8,128)}, u32[]{:S(2)}) copy-start(f32[1,128,1024]{2,1,0:T(8,128)} %param.8) | copy-start | bytes 1572868
  1.8 16.1 %copy-start.3 = (f32[2,27,17]{1,0,2:T(2,128)S(1)}, f32[2,27,17]{1,0,2:T(2,128)}, u32[]{:S(2)}) copy-start(f32[2,27,17]{1,0,2:T(2,128)} %param.10) | copy-start | bytes 11020
  1.8 16.3 %copy-start.2 = (f32[1,9]{1,0:T(1,128)S(1)}, f32[1,9]{1,0:T(1,128)}, u32[]{:S(2)}) copy-start(f32[1,9]{1,0:T(1,128)} %param.12) | copy-start | bytes 112
  1.8 18.0 %all-to-all-start = ((f32[8,16,1024]{2,1,0:T(8,128)}), f32[8,16,1024]{2,1,0:T(8,128)S(1)}, u32[]{:S(2)}, u32[]{:S(2)}) async-start(f32[8,16,1024]{2,1,0:T(8,128)} %broadcast_in_dim.2), calls=%async_computation | async-start | bytes 1048576 | tf_op jit(solution)/shard_map/all_to_all | solution.py:332
  8.1 25.4 %collective-permute-start = (f32[48,1024]{1,0:T(8,128)}, f32[48,1024]{1,0:T(8,128)}, u32[]{:S(2)}, u32[]{:S(2)}) collective-permute-start(f32[48,1024]{1,0:T(8,128)} %get-tuple-element.38), channel_id=1, source_target_pairs={{0,8},{8,16},{16,24},{24,32},{32,40},{40,48},{48,56},{56,64},{64,7... | collective-permute-start | bytes 589832 | tf_op jit(solution)/shard_map/ppermute | solution.py:324
  10.0 23.5 %collective-permute-start.1 = (f32[48,1024]{1,0:T(8,128)}, f32[48,1024]{1,0:T(8,128)}, u32[]{:S(2)}, u32[]{:S(2)}) collective-permute-start(f32[48,1024]{1,0:T(8,128)} %get-tuple-element.37), channel_id=1, source_target_pairs={{8,0},{16,8},{24,16},{32,24},{40,32},{48,40},{56,48},{64,56},{72,6... | collective-permute-start | bytes 589832 | tf_op jit(solution)/shard_map/ppermute | solution.py:325
  19.9 13.6 %collective-permute-start.2 = (f32[32,1024]{1,0:T(8,128)S(1)}, f32[32,1024]{1,0:T(8,128)S(1)}, u32[]{:S(2)}, u32[]{:S(2)}) collective-permute-start(f32[32,1024]{1,0:T(8,128)S(1)} %bitcast.40), channel_id=1, source_target_pairs={{0,8},{8,16},{16,24},{24,32},{32,40},{40,48},{48,56},{56,64},{64,7... | collective-permute-start | bytes 393224 | tf_op jit(solution)/shard_map/ppermute | solution.py:324
  21.8 11.7 %collective-permute-start.3 = (f32[32,1024]{1,0:T(8,128)S(1)}, f32[32,1024]{1,0:T(8,128)S(1)}, u32[]{:S(2)}, u32[]{:S(2)}) collective-permute-start(f32[32,1024]{1,0:T(8,128)S(1)} %bitcast.39), channel_id=1, source_target_pairs={{8,0},{16,8},{24,16},{32,24},{40,32},{48,40},{56,48},{64,56},{72,6... | collective-permute-start | bytes 393224 | tf_op jit(solution)/shard_map/ppermute | solution.py:325
  39.1 5.7 %copy-start.4 = (s32[1,24,8,2]{1,3,2,0:T(2,128)S(1)}, s32[1,24,8,2]{1,3,2,0:T(2,128)}, u32[]{:S(2)}) copy-start(s32[1,24,8,2]{1,3,2,0:T(2,128)} %param.14) | copy-start | bytes 4612
  39.1 15.7 %all-to-all-start.1 = ((bf16[8,56,1024]{2,1,0:T(8,128)(2,1)}), bf16[8,56,1024]{2,1,0:T(8,128)(2,1)S(1)}, u32[]{:S(2)}, u32[]{:S(2)}) async-start(bf16[8,56,1024]{2,1,0:T(8,128)(2,1)} %outer.1), calls=%async_computation.1 | async-start | bytes 1835008 | tf_op jit(solution)/shard_map/all_to_all | solution.py:404

commit v3 on v2

--- a/solution.py
+++ b/solution.py
@@ -159,6 +159,14 @@
     for k in range(1, PTAPS):
         power = power + psf[k] * psf[k]
     weight[...] = jnp.full((8, 128), power * power * (jnp.sum(inv_var[...]) / (H * W)), f32)
+
+
+def repeat_kernel(band, out, sems):
+    copies = [pltpu.make_async_copy(band, out.at[e], sems.at[e]) for e in range(EPOCHS)]
+    for copy in copies:
+        copy.start()
+    for copy in copies:
+        copy.wait()
 
 
 def inner_kernel(bands, lhs, visits, inv_var, row_filter, col_filter,
@@ -328,8 +336,16 @@
 
 def on_device(visits, template, basis_taps, coeffs, psf_taps, inv_var, shifts, vel_count):
     visits, inv_var, psf = visits[0], inv_var[0], psf_taps[0]
-    epochs = lax.axis_size("epoch")
-    bands = lax.all_to_all(jnp.broadcast_to(template[None], (epochs, BAND, W)), "epoch", 0, 0, tiled=True)
+    copies = pl.pallas_call(
+        repeat_kernel,
+        out_shape=shape(EPOCHS, BAND, W),
+        in_specs=[pl.BlockSpec(memory_space=pl.ANY)],
+        out_specs=pl.BlockSpec(memory_space=pl.ANY),
+        scratch_shapes=[pltpu.SemaphoreType.DMA((EPOCHS,))],
+        compiler_params=pltpu.CompilerParams(vmem_limit_bytes=1 << 20),
+        name="repeat",
+    )(pltpu.with_memory_space_constraint(template, pltpu.HBM))
+    bands = lax.all_to_all(copies, "epoch", 0, 0, tiled=True)
     own = jnp.pad(coeffs[0, 0].T, ((0, 5), (0, 128 - NB)))
     wide = jnp.pad(own, ((0, 0), (0, W - 128)))
     above, below = to_neighbours(

time: 59.2 us -> 76.5 us (1.29)
  the two profiles are of different devices: /device:TPU:256 before, /device:TPU:249 now
where the time goes in v3:
time: 76.5 us; the launch traced here: 76.1 us
  Pallas kernels  32.6 us (43%)
  starting transfers between devices  29.1 us (38%)
  waiting for transfers between devices  12.1 us (16%)
  between operations  0.89 us (1%)
  other arithmetic  0.8 us (1%)
    pallas_call x1, Pallas kernels, on_device(): pl.pallas_call(repeat_kernel, out_shape=shape(EPOCHS, BAND, W), in_specs=...  17.1 us
    ppermute x2, starting transfers between devices, to_neighbours(): lax.ppermute(downward, 'sky', [(i, i + 1) for i in range(tiles - 1)])  14.4 us
    all_to_all x1, waiting for transfers between devices, on_device(): moved = lax.all_to_all(windows, 'epoch', 0, 0, tiled=True)  7.34 us
    all_to_all x1, starting transfers between devices, on_device(): moved = lax.all_to_all(windows, 'epoch', 0, 0, tiled=True)  5.66 us
    pallas_call x1, Pallas kernels, on_device(): pl.pallas_call(outer_kernel, out_shape=shape(EPOCHS, OUTR, W, dtype=bf16)...  5.55 us
    all_to_all x1, starting transfers between devices, on_device(): bands = lax.all_to_all(copies, 'epoch', 0, 0, tiled=True)  5.21 us
    ppermute x2, waiting for transfers between devices, to_neighbours(): below = lax.ppermute(upward, 'sky', [(i + 1, i) for i in range(tiles - 1)])  4.72 us
    pallas_call x1, Pallas kernels, on_device(): pl.pallas_call(search_kernel, out_shape=shape(BAND, W), in_specs=smem(3)...  4.45 us
  transfers between devices with their start and end apart: 6, of which 2 were waited for; matrix products, arithmetic and copies ran while one was open for 2% of the time, Pallas kernels for 7%

profile of v3, /device:TPU:249, one launch (start us, length us, event | category | flops | bytes accessed | tf_op | source)
XLA Modules:
  0.0 76.1 jit_solution(14565829085569377756)
XLA Ops:
  0.0 0.0 copy-start.5
  0.0 0.0 copy-start
  0.0 0.0 copy-start.1
  0.0 17.1 %repeat.1 = f32[8,16,1024]{2,1,0:T(8,128)} custom-call(f32[16,1024]{1,0:T(8,128)} %band.1), custom_call_target="tpu_custom_call" | custom-call | tf_op jit(solution)/shard_map/repeat/pallas_call | solution.py:339
  17.1 0.0 copy-start.3
  17.1 0.0 copy-start.2
  17.1 5.2 %all-to-all-start = ((f32[8,16,1024]{2,1,0:T(8,128)}), f32[8,16,1024]{2,1,0:T(8,128)S(1)}, u32[]{:S(2)}, u32[]{:S(2)}) async-start(f32[8,16,1024]{2,1,0:T(8,128)} %repeat.1), calls=%async_computation | async-start | bytes 1048576 | tf_op jit(solution)/shard_map/all_to_all | solution.py:348
  22.3 0.0 copy-done.5
  22.3 0.0 copy-done
  22.3 0.0 copy-done.1
  22.4 0.8 %fusion.1 = (f32[48,1024]{1,0:T(8,128)}, f32[48,1024]{1,0:T(8,128)}) fusion(f32[8,128]{1,0:T(8,128)S(1)} %pad.16.coeffs, f32[16,1024]{1,0:T(8,128)S(1)} %get-tuple-element.31, f32[24,1024]{1,0:T(8,128)S(1)} %get-tuple-element.29, f32[16,1024]{1,0:T(8,128)S(1)} %get-tuple-element.32, f32[24,1024]{1,0:T(8,128)S(1)} %get-tuple-element.30), kind=kLoop, calls=%fused_computation.3 | loop fusion | flops 294912 | bytes 724992 | tf_op jit(solution)/shard_map/concatenate | solution.py:353
  23.2 6.5 %collective-permute-start = (f32[48,1024]{1,0:T(8,128)}, f32[48,1024]{1,0:T(8,128)}, u32[]{:S(2)}, u32[]{:S(2)}) collective-permute-start(f32[48,1024]{1,0:T(8,128)} %get-tuple-element.38), channel_id=1, source_target_pairs={{0,8},{8,16},{16,24},{24,32},{32,40},{40,48},{48,56},{56,64},{64,7... | collective-permute-start | bytes 589832 | tf_op jit(solution)/shard_map/ppermute | solution.py:332
  29.7 1.9 %collective-permute-start.1 = (f32[48,1024]{1,0:T(8,128)}, f32[48,1024]{1,0:T(8,128)}, u32[]{:S(2)}, u32[]{:S(2)}) collective-permute-start(f32[48,1024]{1,0:T(8,128)} %get-tuple-element.37), channel_id=1, source_target_pairs={{8,0},{16,8},{24,16},{32,24},{40,32},{48,40},{56,48},{64,56},{72,6... | collective-permute-start | bytes 589832 | tf_op jit(solution)/shard_map/ppermute | solution.py:333
  31.6 0.0 copy-done.3
  31.7 0.1 copy.23
  31.8 0.0 copy-done.2
  31.8 1.7 %prepare.1 = (bf16[2,224,1360]{2,1,0:T(8,128)(2,1)S(1)}, f32[8,128]{1,0:T(8,128)S(1)}, bf16[192,112]{1,0:T(8,128)(2,1)S(1)}, bf16[64,48]{1,0:T(8,128)(2,1)S(1)}, bf16[2,512,256]{2,1,0:T(8,128)(2,1)S(1)}) custom-call(f32[9]{0:T(128)S(1)} %bitcast.38, f32[128,1024]{1,0:T(8,128)S(1)} %bitcast.33, f32[8,128]{1,0:T(8,128)S(1)} %pad.16.coeffs, ...), custom_call_target="tpu_custom_call" | custom-call | tf_op jit(solution)/shard_map/prepare/pallas_call | solution.py:357
  33.6 0.0 all-to-all-done.bands
  33.6 7.9 %collective-permute-start.2 = (f32[32,1024]{1,0:T(8,128)S(1)}, f32[32,1024]{1,0:T(8,128)S(1)}, u32[]{:S(2)}, u32[]{:S(2)}) collective-permute-start(f32[32,1024]{1,0:T(8,128)S(1)} %bitcast.40), channel_id=1, source_target_pairs={{0,8},{8,16},{16,24},{24,32},{32,40},{40,48},{48,56},{56,64},{64,7... | collective-permute-start | bytes 393224 | tf_op jit(solution)/shard_map/ppermute | solution.py:332
  41.5 1.9 %collective-permute-start.3 = (f32[32,1024]{1,0:T(8,128)S(1)}, f32[32,1024]{1,0:T(8,128)S(1)}, u32[]{:S(2)}, u32[]{:S(2)}) collective-permute-start(f32[32,1024]{1,0:T(8,128)S(1)} %bitcast.39), channel_id=1, source_target_pairs={{8,0},{16,8},{24,16},{32,24},{40,32},{48,40},{56,48},{64,56},{72,6... | collective-permute-start | bytes 393224 | tf_op jit(solution)/shard_map/ppermute | solution.py:333
  43.4 3.8 %inner.1 = (bf16[96,1024]{1,0:T(8,128)(2,1)S(1)}, f32[32,1024]{1,0:T(8,128)S(1)}, bf16[17,32,1024]{2,1,0:T(8,128)(2,1)S(1)}, bf16[17,32,1024]{2,1,0:T(8,128)(2,1)S(1)}) custom-call(f32[8,16,1024]{2,1,0:T(8,128)S(1)} %all-to-all-done.bands, bf16[2,224,1360]{2,1,0:T(8,128)(2,1)S(1)} %get-tuple-element.18.lhs, f32[128,1024]{1,0:T(8,128)S(1)} %bitcast.36, ...), custom_call_target="tpu_custom_call" | custom-call | tf_op jit(solution)/shard_map/inner/pallas_call | solution.py:378
  47.2 0.0 collective-permute-done.above
  47.2 0.0 collective-permute-done.1.below
  47.2 0.0 collective-permute-done.2.t_above
  47.2 4.7 %collective-permute-done.3.t_below = f32[32,1024]{1,0:T(8,128)S(1)} collective-permute-done((f32[32,1024]{1,0:T(8,128)S(1)}, f32[32,1024]{1,0:T(8,128)S(1)}, u32[]{:S(2)}, u32[]{:S(2)}) %collective-permute-start.3) | collective-permute-done | bytes 131104 | tf_op jit(solution)/shard_map/ppermute | solution.py:333
  52.0 5.6 %outer.1 = bf16[8,56,1024]{2,1,0:T(8,128)(2,1)} custom-call(f32[128,1024]{1,0:T(8,128)S(1)} %bitcast.37, f32[128,1024]{1,0:T(8,128)S(1)} %bitcast.35, f32[48,1024]{1,0:T(8,128)} %collective-permute-done.above, f32[48,1024]{1,0:T(8,128)} %collective-permute-done.1.below, f32[32,1024]{1,0:T(8,128)S(1)} %collective-permute-done.2.t_above, ...), custom_call_target="tpu_custom_call" | custom-call | tf_op jit(solution)/shard_map/outer/pallas_call | solution.py:397
  57.5 0.0 copy-start.4
  57.5 5.7 %all-to-all-start.1 = ((bf16[8,56,1024]{2,1,0:T(8,128)(2,1)}), bf16[8,56,1024]{2,1,0:T(8,128)(2,1)S(1)}, u32[]{:S(2)}, u32[]{:S(2)}) async-start(bf16[8,56,1024]{2,1,0:T(8,128)(2,1)} %outer.1), calls=%async_computation.1 | async-start | bytes 1835008 | tf_op jit(solution)/shard_map/all_to_all | solution.py:420
  63.2 0.0 copy-done.4
  63.2 0.1 copy.16
  63.3 0.1 add.37
  63.4 0.1 add.34
  63.5 0.1 copy.17
  63.6 0.1 reshape_squeeze.3.across_of
  64.3 7.3 %all-to-all-done.1.windows = bf16[8,56,1024]{2,1,0:T(8,128)(2,1)S(1)} async-done(((bf16[8,56,1024]{2,1,0:T(8,128)(2,1)}), bf16[8,56,1024]{2,1,0:T(8,128)(2,1)S(1)}, u32[]{:S(2)}, u32[]{:S(2)}) %all-to-all-start.1) | async-done | bytes 917536 | tf_op jit(solution)/shard_map/all_to_all | solution.py:420
  71.7 4.5 %search.1 = f32[16,1024]{1,0:T(8,128)} custom-call(s32[1]{0:T(128)S(6)} %copy.28.count, s32[192]{0:T(256)S(1)} %fusion.3.starts, s32[192]{0:T(256)S(1)} %reshape_squeeze.3.across_of, bf16[8,56,1024]{2,1,0:T(8,128)(2,1)S(1)} %all-to-all-done.1.windows), custom_call_target="tpu_custom_call" | custom-call | tf_op jit(solution)/shard_map/search/pallas_call | solution.py:421
  (14 shorter events, 0.1 us)
Async XLA Ops:
  0.0 22.3 %copy-start.5 = (f32[1,1,27,3]{2,1,3,0:T(1,128)S(1)}, f32[1,1,27,3]{2,1,3,0:T(1,128)}, u32[]{:S(2)}) copy-start(f32[1,1,27,3]{2,1,3,0:T(1,128)} %param.11) | copy-start | bytes 976
  0.0 22.3 %copy-start = (f32[1,128,1024]{2,1,0:T(8,128)S(1)}, f32[1,128,1024]{2,1,0:T(8,128)}, u32[]{:S(2)}) copy-start(f32[1,128,1024]{2,1,0:T(8,128)} %param.13) | copy-start | bytes 1572868
  0.0 22.3 %copy-start.1 = (f32[1,128,1024]{2,1,0:T(8,128)S(1)}, f32[1,128,1024]{2,1,0:T(8,128)}, u32[]{:S(2)}) copy-start(f32[1,128,1024]{2,1,0:T(8,128)} %param.8) | copy-start | bytes 1572868
  17.1 14.6 %copy-start.3 = (f32[2,27,17]{1,0,2:T(2,128)S(1)}, f32[2,27,17]{1,0,2:T(2,128)}, u32[]{:S(2)}) copy-start(f32[2,27,17]{1,0,2:T(2,128)} %param.10) | copy-start | bytes 11020
  17.1 14.7 %copy-start.2 = (f32[1,9]{1,0:T(1,128)S(1)}, f32[1,9]{1,0:T(1,128)}, u32[]{:S(2)}) copy-start(f32[1,9]{1,0:T(1,128)} %param.12) | copy-start | bytes 112
  17.1 16.5 %all-to-all-start = ((f32[8,16,1024]{2,1,0:T(8,128)}), f32[8,16,1024]{2,1,0:T(8,128)S(1)}, u32[]{:S(2)}, u32[]{:S(2)}) async-start(f32[8,16,1024]{2,1,0:T(8,128)} %repeat.1), calls=%async_computation | async-start | bytes 1048576 | tf_op jit(solution)/shard_map/all_to_all | solution.py:348
  23.2 24.0 %collective-permute-start = (f32[48,1024]{1,0:T(8,128)}, f32[48,1024]{1,0:T(8,128)}, u32[]{:S(2)}, u32[]{:S(2)}) collective-permute-start(f32[48,1024]{1,0:T(8,128)} %get-tuple-element.38), channel_id=1, source_target_pairs={{0,8},{8,16},{16,24},{24,32},{32,40},{40,48},{48,56},{56,64},{64,7... | collective-permute-start | bytes 589832 | tf_op jit(solution)/shard_map/ppermute | solution.py:332
  29.7 17.5 %collective-permute-start.1 = (f32[48,1024]{1,0:T(8,128)}, f32[48,1024]{1,0:T(8,128)}, u32[]{:S(2)}, u32[]{:S(2)}) collective-permute-start(f32[48,1024]{1,0:T(8,128)} %get-tuple-element.37), channel_id=1, source_target_pairs={{8,0},{16,8},{24,16},{32,24},{40,32},{48,40},{56,48},{64,56},{72,6... | collective-permute-start | bytes 589832 | tf_op jit(solution)/shard_map/ppermute | solution.py:333
  33.6 13.6 %collective-permute-start.2 = (f32[32,1024]{1,0:T(8,128)S(1)}, f32[32,1024]{1,0:T(8,128)S(1)}, u32[]{:S(2)}, u32[]{:S(2)}) collective-permute-start(f32[32,1024]{1,0:T(8,128)S(1)} %bitcast.40), channel_id=1, source_target_pairs={{0,8},{8,16},{16,24},{24,32},{32,40},{40,48},{48,56},{56,64},{64,7... | collective-permute-start | bytes 393224 | tf_op jit(solution)/shard_map/ppermute | solution.py:332
  41.5 10.5 %collective-permute-start.3 = (f32[32,1024]{1,0:T(8,128)S(1)}, f32[32,1024]{1,0:T(8,128)S(1)}, u32[]{:S(2)}, u32[]{:S(2)}) collective-permute-start(f32[32,1024]{1,0:T(8,128)S(1)} %bitcast.39), channel_id=1, source_target_pairs={{8,0},{16,8},{24,16},{32,24},{40,32},{48,40},{56,48},{64,56},{72,6... | collective-permute-start | bytes 393224 | tf_op jit(solution)/shard_map/ppermute | solution.py:333
  57.5 5.7 %copy-start.4 = (s32[1,24,8,2]{1,3,2,0:T(2,128)S(1)}, s32[1,24,8,2]{1,3,2,0:T(2,128)}, u32[]{:S(2)}) copy-start(s32[1,24,8,2]{1,3,2,0:T(2,128)} %param.14) | copy-start | bytes 4612
  57.5 14.1 %all-to-all-start.1 = ((bf16[8,56,1024]{2,1,0:T(8,128)(2,1)}), bf16[8,56,1024]{2,1,0:T(8,128)(2,1)S(1)}, u32[]{:S(2)}, u32[]{:S(2)}) async-start(bf16[8,56,1024]{2,1,0:T(8,128)(2,1)} %outer.1), calls=%async_computation.1 | async-start | bytes 1835008 | tf_op jit(solution)/shard_map/all_to_all | solution.py:420
